TPU v7x, 128 devices: a whole 4x4x4 slice. The times are simulated.
128 devices in a mesh: dp: 8 (over z, core), tensor: 16 (over x, y).
Axes of the slice: x: 4, y: 4, z: 4, core: 2. Of those that a mesh axis runs over, the one named last changes fastest.
Arguments:
- residual_in: bfloat16 [1024, 4096], P('dp'), may hold values from -3 to 3
- query: bfloat16 [1024, 8192], P('dp', 'tensor'), may hold values from -130 to 130
- fresh_key: bfloat16 [1024, 4, 128], P('dp'), may hold values from -5 to 5
- fresh_value: bfloat16 [1024, 4, 128], P('dp'), may hold values from -10 to 10
- key_cache: bfloat16 [1024, 16, 128, 128], P('dp', 'tensor'), may hold values from -5 to 5, as said below
- value_cache: bfloat16 [1024, 16, 128, 128], P('dp', 'tensor'), may hold values from -10 to 10, as said below
- lengths: int32 [1024], P('dp'), may hold values from 2 to 128
- out_weight: bfloat16 [8192, 4096], P('tensor'), may hold values from -0.0625 to 0.0625
- norm_gain: float32 [4096], replicated, may hold values from 0.1 to 1.9
- expert_ids: int32 [1024, 8], P('dp'), may hold values from 0 to 127, all different within a row; in each aligned block of 128 rows (0 to 127, 128 to 255, ...) at most 16 rows name the same one
- gate_scores: float32 [1024, 8], P('dp'), may hold values from 0.05 to 1
- w_gate: bfloat16 [128, 4096, 768], P(('dp', 'tensor')), may hold values from -0.09375 to 0.09375
- w_up: bfloat16 [128, 4096, 768], P(('dp', 'tensor')), may hold values from -0.09375 to 0.09375
- w_down: bfloat16 [128, 768, 4096], P(('dp', 'tensor')), may hold values from -0.21875 to 0.21875
Outputs:
- layer_out: bfloat16 [1024, 4096], P(('dp', 'tensor'))
Inputs may be any that keep to these rules, and one draw needn't show every extreme that they name: `expert_ids`: each row names 8 different experts; among the 128 rows of one data replica (aligned blocks) no expert is named by more than 16 rows, a bound that some block reaches. `key_cache`: the copies of one key head are equal. `value_cache`: the copies of one value head are equal.
All inputs are finite; a program needn't handle non-finite values.
Results may differ from a plain program's by a relative error of at most 0.023.
Values may be sent and summed in bfloat16 or wider, within the bound.
No kernel may reach another device: no remote copies, remote signals or barrier semaphores. Data moves between devices by JAX's collectives and lax.ppermute only.
A program may use at most 128 MiB of HBM per device.

v0:
```python
import jax
import jax.numpy as jnp
from jax import lax
from jax.sharding import PartitionSpec as P


def rms_normalize(hidden, norm_gain):
    widened = hidden.astype(jnp.float32)
    spread = jnp.mean(widened * widened, axis=-1, keepdims=True)
    return (widened * lax.rsqrt(spread + 1e-06) * norm_gain).astype(jnp.bfloat16)


def shards(
    residual_in,
    query,
    fresh_key,
    fresh_value,
    key_cache,
    value_cache,
    lengths,
    out_weight,
    norm_gain,
    expert_ids,
    gate_scores,
    w_gate,
    w_up,
    w_down,
):
    row_count = residual_in.shape[0]
    head_size = key_cache.shape[3]
    tensor_width = lax.axis_size("tensor")
    column = lax.axis_index("tensor")
    kv_head = column // (tensor_width // fresh_key.shape[1])
    head_count = query.shape[1] // head_size
    score_scale = head_size ** (-0.5)
    query_rows = query.reshape(row_count, head_count, head_size)
    cached_keys = key_cache[:, 0]
    cached_values = value_cache[:, 0]
    own_key = lax.dynamic_index_in_dim(fresh_key, kv_head, 1, keepdims=False)
    own_value = lax.dynamic_index_in_dim(fresh_value, kv_head, 1, keepdims=False)
    scores = (
        jnp.einsum("rhd,rpd->rhp", query_rows, cached_keys, preferred_element_type=jnp.float32)
        * score_scale
    )
    own_score = (
        jnp.einsum("rhd,rd->rh", query_rows, own_key, preferred_element_type=jnp.float32)
        * score_scale
    )
    in_cache = (
        lax.broadcasted_iota(jnp.int32, (row_count, cached_keys.shape[1]), 1) < lengths[:, None]
    )
    scores = jnp.where(in_cache[:, None, :], scores, -1e30)
    row_max = jnp.maximum(jnp.max(scores, axis=-1), own_score)
    cache_terms = jnp.exp(scores - row_max[..., None])
    own_term = jnp.exp(own_score - row_max)
    denom = jnp.sum(cache_terms, axis=-1) + own_term
    probs = (cache_terms / denom[..., None]).astype(jnp.bfloat16)
    own_prob = (own_term / denom).astype(jnp.bfloat16)
    attended = jnp.einsum("rhp,rpd->rhd", probs, cached_values, preferred_element_type=jnp.float32)
    attended = (
        attended
        + own_prob.astype(jnp.float32)[..., None] * own_value.astype(jnp.float32)[:, None, :]
    )
    heads_out = attended.astype(jnp.bfloat16).reshape(row_count, head_count * head_size)
    share_rows = row_count // tensor_width
    first_own = column * share_rows
    proj = lax.psum(
        jnp.dot(heads_out, out_weight, preferred_element_type=jnp.float32).astype(jnp.bfloat16),
        "tensor",
    ).astype(jnp.float32)
    hidden_all = (residual_in.astype(jnp.float32) + proj).astype(jnp.bfloat16)
    normed = rms_normalize(hidden_all, norm_gain)
    hidden_own = lax.dynamic_slice_in_dim(hidden_all, first_own, share_rows, 0)
    replica_count = lax.axis_size("dp")
    experts_all = replica_count * tensor_width
    topk_count = expert_ids.shape[1]
    cap_slots = 2 * max(1, row_count * topk_count // experts_all)
    targets = lax.broadcasted_iota(jnp.int32, (replica_count,), 0) * tensor_width + column
    matches = expert_ids[:, :, None] == targets[None, None, :]
    weights = gate_scores / jnp.sum(gate_scores, axis=1, keepdims=True)
    routed = jnp.any(matches, axis=1)
    picked_weight = jnp.sum(jnp.where(matches, weights[:, :, None], 0.0), axis=1)
    slot_index = jnp.cumsum(routed.astype(jnp.int32), axis=0) - 1
    slot_ids = lax.broadcasted_iota(jnp.int32, (1, cap_slots, 1), 1)
    selector = ((slot_index.T[:, None, :] == slot_ids) & routed.T[:, None, :]).astype(jnp.bfloat16)
    outgoing = jnp.einsum(
        "bcr,rd->bcd", selector, normed, preferred_element_type=jnp.float32
    ).astype(jnp.bfloat16)
    received = lax.all_to_all(outgoing, "dp", split_axis=0, concat_axis=0, tiled=True)
    flat_rows = received.reshape(-1, received.shape[2])
    gate_part = jnp.dot(flat_rows, w_gate[0], preferred_element_type=jnp.float32)
    up_part = jnp.dot(flat_rows, w_up[0], preferred_element_type=jnp.float32)
    act = (jax.nn.silu(gate_part) * up_part).astype(jnp.bfloat16)
    result = jnp.dot(act, w_down[0], preferred_element_type=jnp.float32).astype(jnp.bfloat16)
    answered = result.reshape(received.shape)
    returned_rows = lax.all_to_all(answered, "dp", split_axis=0, concat_axis=0, tiled=True)
    gathered = jnp.einsum(
        "bcr,bcd->brd", selector, returned_rows, preferred_element_type=jnp.float32
    )
    mixture_own = lax.psum_scatter(
        jnp.sum(picked_weight.T[:, :, None] * gathered, axis=0).astype(jnp.bfloat16),
        "tensor",
        scatter_dimension=0,
        tiled=True,
    ).astype(jnp.float32)
    return (hidden_own.astype(jnp.float32) + mixture_own).astype(jnp.bfloat16)


def solution(mesh):
    placed = (
        P("dp", None),
        P("dp", "tensor"),
        P("dp", None, None),
        P("dp", None, None),
        P("dp", "tensor", None, None),
        P("dp", "tensor", None, None),
        P("dp"),
        P("tensor", None),
        P(),
        P("dp", None),
        P("dp", None),
        P(("dp", "tensor"), None, None),
        P(("dp", "tensor"), None, None),
        P(("dp", "tensor"), None, None),
    )
    return jax.shard_map(
        shards, mesh=mesh, in_specs=placed, out_specs=P(("dp", "tensor"), None), check_vma=False
    )
```

profile of v0, /device:TPU:0, one launch (start us, length us, event | category | flops | bytes accessed | tf_op | source)
XLA Modules:
  0.0 260.0 jit_solution(1109410905941494168)
XLA Ops:
  6.5 1.1 dynamic-slice_convert_fusion
  7.6 0.9 reshape.50
  8.6 0.3 fusion.54
  8.9 0.8 iota_compare_fusion.1
  9.7 4.5 %fusion.65 = (f32[128,4]{1,0:T(8,128)S(1)}, f32[128,4,128]{2,1,0:T(4,128)S(1)}) fusion(bf16[128,4,128]{2,1,0:T(4,128)(2,1)S(1)} %reshape.50, bf16[128,1,128,128]{3,2,1,0:T(8,128)(2,1)} %param.18, pred[128,128]{1,0:T(8,128)(4,1)S(1)} %iota_compare_fusion.1), kind=kOutput, calls=%fused_computation.69 | convolution fusion | flops 16973312 | bytes 4605952 | tf_op jit(solution)/shard_map/rhd,rpd->rhp/dot_general | solution.py:42
  14.3 0.1 copy.40
  14.4 0.4 fusion.45
  14.9 0.1 copy.42
  15.0 0.1 copy.43
  15.2 3.6 %fusion.31 = bf16[128,4,128]{2,1,0:T(4,128)(2,1)S(1)} fusion(bf16[128,1,128,128]{3,2,1,0:T(8,128)(2,1)} %param.19, f32[128,4,128]{2,1,0:T(4,128)S(1)} %get-tuple-element.10, f32[128,128]{1,0:T(8,128)S(1)} %bitcast.77, f32[128,4]{1,0:T(8,128)S(1)} %copy.43, f32[128,4]{1,0:T(8,128)S(1)} %copy.42, f32[128,4]{1,0:T(8,128)S(1)} %copy.40), kind=kOutput, calls=%fused_computation.25 | convolution fusion | flops 17170432 | bytes 4659200 | tf_op jit(solution)/shard_map/rhp,rpd->rhd/dot_general | solution.py:59
  18.8 1.8 convolution_convert_fusion.1
  20.8 0.2 reduce_window_sum.11
  21.0 89.0 %all-reduce.4.cloned.1.call-done = bf16[128,4096]{1,0:T(8,128)(2,1)} async-done(((bf16[128,4096]{1,0:T(8,128)(2,1)}), bf16[128,4096]{1,0:T(8,128)(2,1)}) %all-reduce.4.cloned.1.call-update) | async-done | bytes 1048592 | tf_op jit(solution)/shard_map/psum | solution.py:67
  110.1 1.7 fusion.13
  111.8 0.5 convolution_convert_fusion
  112.3 20.3 %all_to_all.10 = bf16[8,16,4096]{2,1,0:T(8,128)(2,1)S(1)} all-to-all(bf16[8,16,4096]{2,1,0:T(8,128)(2,1)S(1)} %convolution_convert_fusion), channel_id=1, replica_groups=mesh['dp'=8,'tensor'=16] {'dp'}, dimensions={0} | all-to-all | bytes 2097152 | tf_op jit(solution)/shard_map/all_to_all | solution.py:89
  132.6 3.8 %fusion.4 = f32[128,768]{1,0:T(8,128)S(1)} fusion(bf16[128,4096]{1,0:T(8,128)(2,1)S(1)} %bitcast.74, bf16[1,4096,768]{2,1,0:T(8,128)(2,1)} %param.25), kind=kOutput, calls=%fused_computation.5 | convolution fusion | flops 805306368 | bytes 7733248 | tf_op jit(solution)/shard_map/dot_general | solution.py:91
  136.4 8.1 %fusion.6 = bf16[128,4096]{1,0:T(8,128)(2,1)} fusion(bf16[1,768,4096]{2,1,0:T(8,128)(2,1)} %param.27, bf16[128,4096]{1,0:T(8,128)(2,1)S(1)} %bitcast.75, bf16[1,4096,768]{2,1,0:T(8,128)(2,1)} %param.26, f32[128,768]{1,0:T(8,128)S(1)} %fusion.4), kind=kOutput, calls=%fused_computation.7 | convolution fusion | flops 1611726848 | bytes 15073280 | tf_op jit(solution)/shard_map/dot_general | solution.py:94
  144.5 3.6 %all-to-all-start.1 = ((bf16[8,16,4096]{2,1,0:T(8,128)(2,1)}), bf16[8,16,4096]{2,1,0:T(8,128)(2,1)S(1)}, u32[]{:S(2)}, u32[]{:S(2)}) async-start(bf16[8,16,4096]{2,1,0:T(8,128)(2,1)} %bitcast.14), calls=%async_computation.1 | async-start | bytes 2097152 | tf_op jit(solution)/shard_map/all_to_all | solution.py:96
  148.2 15.7 %all-to-all-done.1 = bf16[8,16,4096]{2,1,0:T(8,128)(2,1)S(1)} async-done(((bf16[8,16,4096]{2,1,0:T(8,128)(2,1)}), bf16[8,16,4096]{2,1,0:T(8,128)(2,1)S(1)}, u32[]{:S(2)}, u32[]{:S(2)}) %all-to-all-start.1) | async-done | bytes 1048608 | tf_op jit(solution)/shard_map/all_to_all | solution.py:96
  163.9 3.5 %multiply_reduce_fusion = bf16[128,4096]{1,0:T(8,128)(2,1)} fusion(bf16[8,16,4096]{2,1,0:T(8,128)(2,1)S(1)} %all-to-all-done.1, f32[8,128]{1,0:T(8,128)S(1)} %bitcast.81, s32[8,128]{1,0:T(8,128)S(1)} %copy.45, pred[8,128]{1,0:T(8,128)(4,1)S(1)} %bitcast.80), kind=kOutput, calls=%fused_computation | convolution fusion | flops 142114816 | bytes 2106368 | tf_op jit(solution)/shard_map/bcr,bcd->brd/dot_general | solution.py:97
  167.4 0.6 dynamic-slice
  168.7 83.0 %all-reduce.6.cloned.1.call-done = bf16[128,4096]{1,0:T(8,128)(2,1)} async-done(((bf16[128,4096]{1,0:T(8,128)(2,1)}), bf16[128,4096]{1,0:T(8,128)(2,1)}) %all-reduce.6.cloned.1.call-update) | async-done | bytes 1048592
  251.6 1.5 add_convert_fusion.1
  (32 shorter events, 0.7 us)
Async XLA Ops:
  6.5 103.5 %all-reduce.4.cloned.1.call-start = ((), (), s32[]{:S(2)}) async-start(), calls=%async_computation.2 | async-start | bytes 2097152 | tf_op jit(solution)/shard_map/psum | solution.py:67
  15.2 3.6 %copy-start = (bf16[512,4096]{1,0:T(8,128)(2,1)S(1)}, bf16[512,4096]{1,0:T(8,128)(2,1)}, u32[]{:S(2)}) copy-start(bf16[512,4096]{1,0:T(8,128)(2,1)} %param.21) | copy-start | bytes 12582916
  18.8 1.8 copy-start.3
  18.8 91.3 %copy-start.1 = (bf16[128,4096]{1,0:T(8,128)(2,1)S(1)}, bf16[128,4096]{1,0:T(8,128)(2,1)}, u32[]{:S(2)}) copy-start(bf16[128,4096]{1,0:T(8,128)(2,1)} %param.14) | copy-start | bytes 3145732
  18.8 93.0 %copy-start.2 = (f32[4096]{0:T(1024)S(1)}, f32[4096]{0:T(1024)}, u32[]{:S(2)}) copy-start(f32[4096]{0:T(1024)} %param.22) | copy-start | bytes 49156
  136.4 11.7 %copy-start.4 = (f32[128,8]{0,1:T(8,128)S(1)}, f32[128,8]{0,1:T(8,128)}, u32[]{:S(2)}) copy-start(f32[128,8]{0,1:T(8,128)} %param.24) | copy-start | bytes 12292
  144.5 19.4 %all-to-all-start.1 = ((bf16[8,16,4096]{2,1,0:T(8,128)(2,1)}), bf16[8,16,4096]{2,1,0:T(8,128)(2,1)S(1)}, u32[]{:S(2)}, u32[]{:S(2)}) async-start(bf16[8,16,4096]{2,1,0:T(8,128)(2,1)} %bitcast.14), calls=%async_computation.1 | async-start | bytes 2097152 | tf_op jit(solution)/shard_map/all_to_all | solution.py:96
  148.0 103.6 %all-reduce.6.cloned.1.call-start = ((), (), s32[]{:S(2)}) async-start(), calls=%async_computation.3 | async-start | bytes 2097152
  163.9 3.5 %copy-start.5 = (u32[128]{0:T(128)S(1)}, u32[128]{0:T(128)}, u32[]{:S(2)}) copy-start(u32[128]{0:T(128)} %constant.65) | copy-start | bytes 1540
Sparse Core Ops, SparseCore 0:
  20.7 89.3 all-reduce.3
  167.6 84.0 all-reduce.5
where the time goes:
time: 260 us
  waiting for transfers between devices  188 us (72%)
  matrix products  26 us (10%)
  blocking collectives  20.3 us (8%)
  between operations  14.2 us (5%)
  other arithmetic  5.8 us (2%)
  starting transfers between devices  3.6 us (1%)
    psum x1, waiting for transfers between devices, shards(): lax.psum(jnp.dot(heads_out, out_weight, preferred_element_type=jnp.float3...  89 us
    unnamed x3, waiting for transfers between devices  83 us
    all_to_all x1, blocking collectives, shards(): lax.all_to_all(outgoing, 'dp', split_axis=0, concat_axis=0, tiled=True)  20.3 us
    all_to_all x1, waiting for transfers between devices, shards(): lax.all_to_all(answered, 'dp', split_axis=0, concat_axis=0, tiled=True)  15.7 us
    dot_general x1, matrix products, shards(): jnp.dot(act, w_down[0], preferred_element_type=jnp.float32)  8.05 us
  transfers between devices with their start and end apart: 3, of which 3 were waited for; matrix products, arithmetic and copies ran while one was open for 0% of the time, Pallas kernels for 0%

commit v1 on v0

v1 whole, which is shorter than its diff:
```python
import jax
import jax.numpy as jnp
from jax import lax
from jax.sharding import PartitionSpec as P


def attend(query, fresh_key, fresh_value, key_cache, value_cache, lengths, column, tensor_width):
    row_count = query.shape[0]
    head_size = key_cache.shape[3]
    kv_head = column // (tensor_width // fresh_key.shape[1])
    head_count = query.shape[1] // head_size
    score_scale = head_size ** (-0.5)
    query_rows = query.reshape(row_count, head_count, head_size)
    cached_keys = key_cache[:, 0]
    cached_values = value_cache[:, 0]
    own_key = lax.dynamic_index_in_dim(fresh_key, kv_head, 1, keepdims=False)
    own_value = lax.dynamic_index_in_dim(fresh_value, kv_head, 1, keepdims=False)
    scores = (
        jnp.einsum("rhd,rpd->rhp", query_rows, cached_keys, preferred_element_type=jnp.float32)
        * score_scale
    )
    own_score = (
        jnp.einsum("rhd,rd->rh", query_rows, own_key, preferred_element_type=jnp.float32)
        * score_scale
    )
    in_cache = (
        lax.broadcasted_iota(jnp.int32, (row_count, cached_keys.shape[1]), 1) < lengths[:, None]
    )
    scores = jnp.where(in_cache[:, None, :], scores, -1e30)
    row_max = jnp.maximum(jnp.max(scores, axis=-1), own_score)
    cache_terms = jnp.exp(scores - row_max[..., None])
    own_term = jnp.exp(own_score - row_max)
    denom = jnp.sum(cache_terms, axis=-1) + own_term
    probs = (cache_terms / denom[..., None]).astype(jnp.bfloat16)
    own_prob = (own_term / denom).astype(jnp.bfloat16)
    attended = jnp.einsum("rhp,rpd->rhd", probs, cached_values, preferred_element_type=jnp.float32)
    attended = (
        attended
        + own_prob.astype(jnp.float32)[..., None] * own_value.astype(jnp.float32)[:, None, :]
    )
    return attended.astype(jnp.bfloat16).reshape(row_count, head_count * head_size)


def route(expert_ids, gate_scores, experts_all):
    row_count = expert_ids.shape[0]
    expert_axis = lax.broadcasted_iota(jnp.int32, (1, 1, experts_all), 2)
    matches = expert_ids[:, :, None] == expert_axis
    weights = gate_scores / jnp.sum(gate_scores, axis=1, keepdims=True)
    row_weight = jnp.sum(jnp.where(matches, weights[:, :, None], 0.0), axis=1).T
    routed = jnp.any(matches, axis=1).astype(jnp.bfloat16).T
    before = (
        lax.broadcasted_iota(jnp.int32, (row_count, row_count), 0)
        < lax.broadcasted_iota(jnp.int32, (row_count, row_count), 1)
    ).astype(jnp.bfloat16)
    rank = jnp.dot(routed, before, preferred_element_type=jnp.float32)
    slot = jnp.where(routed > 0, rank, -1.0).astype(jnp.int32)
    return slot, row_weight


def shards(
    residual_in,
    query,
    fresh_key,
    fresh_value,
    key_cache,
    value_cache,
    lengths,
    out_weight,
    norm_gain,
    expert_ids,
    gate_scores,
    w_gate,
    w_up,
    w_down,
):
    both = ("dp", "tensor")
    row_count, width = residual_in.shape
    tensor_width = lax.axis_size("tensor")
    replica_count = lax.axis_size("dp")
    experts_all = replica_count * tensor_width
    column = lax.axis_index("tensor")
    chunk = width // tensor_width
    cap_slots = 2 * max(1, row_count * expert_ids.shape[1] // experts_all)

    heads_out = attend(
        query, fresh_key, fresh_value, key_cache, value_cache, lengths, column, tensor_width
    )
    partial = jnp.einsum(
        "rk,ktj->trj",
        heads_out,
        out_weight.reshape(-1, tensor_width, chunk),
        preferred_element_type=jnp.float32,
    ).astype(jnp.bfloat16)
    pieces = lax.all_to_all(partial, "tensor", split_axis=0, concat_axis=0, tiled=True)
    proj = jnp.sum(pieces.astype(jnp.float32), axis=0)
    residual = lax.dynamic_slice_in_dim(residual_in, column * chunk, chunk, 1)
    hidden = (residual.astype(jnp.float32) + proj).astype(jnp.bfloat16)

    slot, row_weight = route(expert_ids, gate_scores, experts_all)
    slot_axis = lax.broadcasted_iota(jnp.int32, (1, cap_slots, 1), 1)
    chosen = slot[:, None, :] == slot_axis
    outgoing = jnp.einsum(
        "esr,rj->esj", chosen.astype(jnp.bfloat16), hidden, preferred_element_type=jnp.float32
    ).astype(jnp.bfloat16)
    received = lax.all_to_all(outgoing, both, split_axis=0, concat_axis=0, tiled=True)

    rows = received.reshape(replica_count, tensor_width, cap_slots, chunk)
    rows = rows.transpose(0, 2, 1, 3).reshape(replica_count * cap_slots, width)
    widened = rows.astype(jnp.float32)
    spread = jnp.mean(widened * widened, axis=-1, keepdims=True)
    normed = (widened * lax.rsqrt(spread + 1e-06) * norm_gain).astype(jnp.bfloat16)
    gate_part = jnp.dot(normed, w_gate[0], preferred_element_type=jnp.float32)
    up_part = jnp.dot(normed, w_up[0], preferred_element_type=jnp.float32)
    act = (jax.nn.silu(gate_part) * up_part).astype(jnp.bfloat16)
    result = jnp.dot(act, w_down[0], preferred_element_type=jnp.float32).astype(jnp.bfloat16)
    result = result.reshape(replica_count, cap_slots, tensor_width, chunk).transpose(0, 2, 1, 3)
    answered = result.reshape(experts_all, cap_slots, chunk)
    returned = lax.all_to_all(answered, both, split_axis=0, concat_axis=0, tiled=True)

    spread_weight = jnp.where(chosen, row_weight[:, None, :], 0.0)
    coarse = spread_weight.astype(jnp.bfloat16)
    fine = (spread_weight - coarse.astype(jnp.float32)).astype(jnp.bfloat16)
    mixture = jnp.einsum(
        "esr,esj->rj", coarse, returned, preferred_element_type=jnp.float32
    ) + jnp.einsum("esr,esj->rj", fine, returned, preferred_element_type=jnp.float32)
    layer = (hidden.astype(jnp.float32) + mixture).astype(jnp.bfloat16)
    own = lax.all_to_all(
        layer.reshape(tensor_width, row_count // tensor_width, chunk),
        "tensor",
        split_axis=0,
        concat_axis=0,
        tiled=True,
    )
    return own.transpose(1, 0, 2).reshape(row_count // tensor_width, width)


def solution(mesh):
    placed = (
        P("dp", None),
        P("dp", "tensor"),
        P("dp", None, None),
        P("dp", None, None),
        P("dp", "tensor", None, None),
        P("dp", "tensor", None, None),
        P("dp"),
        P("tensor", None),
        P(),
        P("dp", None),
        P("dp", None),
        P(("dp", "tensor"), None, None),
        P(("dp", "tensor"), None, None),
        P(("dp", "tensor"), None, None),
    )
    return jax.shard_map(
        shards, mesh=mesh, in_specs=placed, out_specs=P(("dp", "tensor"), None), check_vma=False
    )
```

time: 260 us -> 124 us (0.48)
  waiting for transfers between devices: 188 us -> 54.3 us
  starting transfers between devices: 3.6 us -> 19.4 us
  between operations: 14.2 us -> 0.26 us
  blocking collectives: 20.3 us -> 10.9 us
  local copies, waits for them, and re-layouts: 2.26 us -> 6.38 us
    psum x1 -> x0, waiting for transfers between devices: 89 us -> none  [shards(): lax.psum(jnp.dot(heads_out, out_weight, preferred_element_type=jnp.float3...]
    unnamed x3 -> x0, waiting for transfers between devices: 83 us -> none
    all_to_all x1 -> x3, waiting for transfers between devices: 15.7 us -> 54.3 us  [the longest x1 18.8 us: shards(): lax.all_to_all(outgoing, both, split_axis=0, concat_axis=0, tiled=True)]
    all_to_all x1 -> x3, starting transfers between devices: 3.56 us -> 19.4 us  [the longest x1 7.48 us: shards(): lax.all_to_all(outgoing, both, split_axis=0, concat_axis=0, tiled=True)]
    all_to_all x1, blocking collectives: 20.3 us -> 10.9 us  [shards(): lax.all_to_all(layer.reshape(tensor_width, row_count // tensor_width, chu...]
    dot_general x7 -> x9, matrix products: 17.9 us -> 18.2 us  [the longest x1 4.56 us: attend(): jnp.einsum('rhd,rpd->rhp', query_rows, cached_keys, preferred_element_typ...]
  transfers between devices with their start and end apart: 3 -> 3, of which waited for: 3 -> 3; matrix products, arithmetic and copies ran while one was open for 0% -> 1% of each run, Pallas kernels for 0% -> 0%
where the time goes in v1:
time: 124 us; the launch traced here: 123 us
  waiting for transfers between devices  54.3 us (44%)
  matrix products  25.2 us (20%)
  starting transfers between devices  19.4 us (16%)
  blocking collectives  10.9 us (9%)
  other arithmetic  6.64 us (5%)
  local copies, waits for them, and re-layouts  6.38 us (5%)
    all_to_all x1, waiting for transfers between devices, shards(): lax.all_to_all(outgoing, both, split_axis=0, concat_axis=0, tiled=True)  18.8 us
    all_to_all x1, waiting for transfers between devices, shards(): lax.all_to_all(answered, both, split_axis=0, concat_axis=0, tiled=True)  18.6 us
    all_to_all x1, waiting for transfers between devices, shards(): lax.all_to_all(partial, 'tensor', split_axis=0, concat_axis=0, tiled=True)  16.9 us
    all_to_all x1, blocking collectives, shards(): lax.all_to_all(layer.reshape(tensor_width, row_count // tensor_width, chu...  10.9 us
    all_to_all x1, starting transfers between devices, shards(): lax.all_to_all(outgoing, both, split_axis=0, concat_axis=0, tiled=True)  7.48 us
    all_to_all x1, starting transfers between devices, shards(): lax.all_to_all(partial, 'tensor', split_axis=0, concat_axis=0, tiled=True)  7.25 us
    dot_general x1, matrix products, shards(): jnp.dot(act, w_down[0], preferred_element_type=jnp.float32)  7.06 us
    all_to_all x1, starting transfers between devices, shards(): lax.all_to_all(answered, both, split_axis=0, concat_axis=0, tiled=True)  4.63 us
  transfers between devices with their start and end apart: 3, of which 3 were waited for; matrix products, arithmetic and copies ran while one was open for 1% of the time, Pallas kernels for 0%

profile of v1, /device:TPU:0, one launch (start us, length us, event | category | flops | bytes accessed | tf_op | source)
XLA Modules:
  0.0 123.0 jit_solution(7923237757974195395)
XLA Ops:
  0.0 0.7 iota_compare_fusion.4
  0.7 1.1 dynamic-slice_convert_fusion
  1.9 0.9 reshape.81
  3.1 4.6 %fusion.80 = (f32[128,4]{1,0:T(8,128)S(1)}, f32[128,4,128]{2,1,0:T(4,128)S(1)}) fusion(bf16[128,4,128]{2,1,0:T(4,128)(2,1)S(1)} %reshape.81, bf16[128,1,128,128]{3,2,1,0:T(8,128)(2,1)} %param.18, pred[128,128]{1,0:T(8,128)(4,1)S(1)} %iota_compare_fusion.4), kind=kOutput, calls=%fused_computation.86 | convolution fusion | flops 16973312 | bytes 4605952 | tf_op jit(solution)/shard_map/rhd,rpd->rhp/dot_general | solution.py:19
  8.6 3.4 %fusion.40 = bf16[128,4,128]{2,1,0:T(4,128)(2,1)S(1)} fusion(bf16[128,1,128,128]{3,2,1,0:T(8,128)(2,1)} %param.19, f32[128,4,128]{2,1,0:T(4,128)S(1)} %get-tuple-element.8, f32[128,128]{1,0:T(8,128)S(1)} %bitcast.116, f32[128,4]{1,0:T(8,128)S(1)} %copy.81, f32[128,4]{1,0:T(8,128)S(1)} %copy.80, f32[128,4]{1,0:T(8,128)S(1)} %copy.78), kind=kOutput, calls=%fused_computation.30 | convolution fusion | flops 17170432 | bytes 4659200 | tf_op jit(solution)/shard_map/rhp,rpd->rhd/dot_general | solution.py:36
  12.1 3.9 %fusion.22 = bf16[16,128,256]{2,1,0:T(8,128)(2,1)} fusion(bf16[128,512,1]{1,0,2:T(8,128)(2,1)S(1)} %reshape.92, bf16[64,16,8,256]{3,2,1,0:T(8,128)(2,1)} %bitcast.118), kind=kOutput, calls=%fused_computation.24 | convolution fusion | flops 537395200 | bytes 5373952 | tf_op jit(solution)/shard_map/rk,ktj->trj/dot_general | solution.py:88
  16.0 7.2 %all-to-all-start = ((bf16[16,128,256]{2,1,0:T(8,128)(2,1)}), bf16[16,128,256]{2,1,0:T(8,128)(2,1)S(1)}, u32[]{:S(2)}, u32[]{:S(2)}) async-start(bf16[16,128,256]{2,1,0:T(8,128)(2,1)} %fusion.22), calls=%async_computation | async-start | bytes 2097152 | tf_op jit(solution)/shard_map/all_to_all | solution.py:94
  24.1 16.9 %all-to-all-done = bf16[16,128,256]{2,1,0:T(8,128)(2,1)S(1)} async-done(((bf16[16,128,256]{2,1,0:T(8,128)(2,1)}), bf16[16,128,256]{2,1,0:T(8,128)(2,1)S(1)}, u32[]{:S(2)}, u32[]{:S(2)}) %all-to-all-start) | async-done | bytes 1048608 | tf_op jit(solution)/shard_map/all_to_all | solution.py:94
  41.1 0.9 add_convert_fusion
  42.0 0.5 convolution_convert_fusion
  42.5 1.6 %copy.88 = bf16[128,16,256]{2,1,0:T(8,128)(2,1)} copy(bf16[128,16,256]{2,0,1:T(8,128)(2,1)S(1)} %convolution_convert_fusion) | data formatting | bytes 2097152 | tf_op jit(solution)/shard_map/convert_element_type | solution.py:104
  44.1 7.5 %all-to-all-start.1 = ((bf16[128,16,256]{2,1,0:T(8,128)(2,1)}), bf16[128,16,256]{2,1,0:T(8,128)(2,1)S(1)}, u32[]{:S(2)}, u32[]{:S(2)}) async-start(bf16[128,16,256]{2,1,0:T(8,128)(2,1)} %copy.88), calls=%async_computation.1 | async-start | bytes 2097152 | tf_op jit(solution)/shard_map/all_to_all | solution.py:105
  51.6 18.8 %all-to-all-done.1 = bf16[128,16,256]{2,1,0:T(8,128)(2,1)S(1)} async-done(((bf16[128,16,256]{2,1,0:T(8,128)(2,1)}), bf16[128,16,256]{2,1,0:T(8,128)(2,1)S(1)}, u32[]{:S(2)}, u32[]{:S(2)}) %all-to-all-start.1) | async-done | bytes 1048608 | tf_op jit(solution)/shard_map/all_to_all | solution.py:105
  70.7 1.3 %fusion.18 = f32[8,16]{0,1:T(8,128)S(1)} fusion(f32[8,16,16,256]{3,2,1,0:T(8,128)S(1)} %bitcast_convert_fusion), kind=kLoop, calls=%fused_computation.18 | loop fusion | flops 1048448 | bytes 2097664 | tf_op jit(solution)/shard_map/reduce_sum | solution.py:110
  72.1 1.2 fusion.17
  73.7 3.8 %fusion.4 = f32[128,768]{1,0:T(8,128)S(1)} fusion(bf16[128,4096]{1,0:T(8,128)(2,1)S(1)} %bitcast.108, bf16[1,4096,768]{2,1,0:T(8,128)(2,1)} %param.25), kind=kOutput, calls=%fused_computation.4 | convolution fusion | flops 805306368 | bytes 7733248 | tf_op jit(solution)/shard_map/dot_general | solution.py:112
  77.5 7.1 %fusion.6 = bf16[128,4096]{1,0:T(8,128)(2,1)S(1)} fusion(bf16[1,768,4096]{2,1,0:T(8,128)(2,1)} %param.27, bf16[128,4096]{1,0:T(8,128)(2,1)S(1)} %bitcast.109, bf16[1,4096,768]{2,1,0:T(8,128)(2,1)} %param.26, f32[128,768]{1,0:T(8,128)S(1)} %fusion.4), kind=kOutput, calls=%fused_computation.6 | convolution fusion | flops 1611726848 | bytes 15073280 | tf_op jit(solution)/shard_map/dot_general | solution.py:115
  84.9 1.4 %copy.93 = bf16[8,16,16,256]{3,2,1,0:T(8,128)(2,1)} copy(bf16[8,16,16,256]{3,1,2,0:T(8,128)(2,1)S(1)} %bitcast_bitcast_fusion) | data formatting | bytes 2097152 | tf_op jit(solution)/shard_map/transpose | solution.py:116
  86.3 4.6 %all-to-all-start.2 = ((bf16[128,16,256]{2,1,0:T(8,128)(2,1)}), bf16[128,16,256]{2,1,0:T(8,128)(2,1)S(1)}, u32[]{:S(2)}, u32[]{:S(2)}) async-start(bf16[128,16,256]{2,1,0:T(8,128)(2,1)} %bitcast.17), calls=%async_computation.2 | async-start | bytes 2097152 | tf_op jit(solution)/shard_map/all_to_all | solution.py:118
  91.4 18.6 %all-to-all-done.2 = bf16[128,16,256]{2,1,0:T(8,128)(2,1)S(1)} async-done(((bf16[128,16,256]{2,1,0:T(8,128)(2,1)}), bf16[128,16,256]{2,1,0:T(8,128)(2,1)S(1)}, u32[]{:S(2)}, u32[]{:S(2)}) %all-to-all-start.2) | async-done | bytes 1048608 | tf_op jit(solution)/shard_map/all_to_all | solution.py:118
  110.0 0.8 convolution_bitcast_fusion
  110.7 0.7 fusion.46
  111.5 10.9 %all_to_all.20 = bf16[16,8,256]{2,1,0:T(8,128)(2,1)S(1)} all-to-all(bf16[16,8,256]{2,1,0:T(8,128)(2,1)S(1)} %fusion.46), channel_id=1, replica_groups=mesh['dp'=8,'tensor'=16] {'tensor'}, dimensions={0} | all-to-all | bytes 131072 | tf_op jit(solution)/shard_map/all_to_all | solution.py:127
  122.4 0.6 copy.128
  (35 shorter events, 3.8 us)
Async XLA Ops:
  12.1 11.2 %copy-start.2 = (s32[128,8]{0,1:T(8,128)S(1)}, s32[128,8]{0,1:T(8,128)}, u32[]{:S(2)}) copy-start(s32[128,8]{0,1:T(8,128)} %param.23) | copy-start | bytes 12292
  16.0 35.5 %copy-start.1 = (f32[4096]{0:T(1024)S(1)}, f32[4096]{0:T(1024)}, u32[]{:S(2)}) copy-start(f32[4096]{0:T(1024)} %param.22) | copy-start | bytes 49156
  16.0 25.0 %all-to-all-start = ((bf16[16,128,256]{2,1,0:T(8,128)(2,1)}), bf16[16,128,256]{2,1,0:T(8,128)(2,1)S(1)}, u32[]{:S(2)}, u32[]{:S(2)}) async-start(bf16[16,128,256]{2,1,0:T(8,128)(2,1)} %fusion.22), calls=%async_computation | async-start | bytes 2097152 | tf_op jit(solution)/shard_map/all_to_all | solution.py:94
  44.1 26.4 %all-to-all-start.1 = ((bf16[128,16,256]{2,1,0:T(8,128)(2,1)}), bf16[128,16,256]{2,1,0:T(8,128)(2,1)S(1)}, u32[]{:S(2)}, u32[]{:S(2)}) async-start(bf16[128,16,256]{2,1,0:T(8,128)(2,1)} %copy.88), calls=%async_computation.1 | async-start | bytes 2097152 | tf_op jit(solution)/shard_map/all_to_all | solution.py:105
  84.6 6.4 %copy-start = (f32[128,8]{0,1:T(8,128)S(1)}, f32[128,8]{0,1:T(8,128)}, u32[]{:S(2)}) copy-start(f32[128,8]{0,1:T(8,128)} %param.24) | copy-start | bytes 12292
  86.3 23.7 %all-to-all-start.2 = ((bf16[128,16,256]{2,1,0:T(8,128)(2,1)}), bf16[128,16,256]{2,1,0:T(8,128)(2,1)S(1)}, u32[]{:S(2)}, u32[]{:S(2)}) async-start(bf16[128,16,256]{2,1,0:T(8,128)(2,1)} %bitcast.17), calls=%async_computation.2 | async-start | bytes 2097152 | tf_op jit(solution)/shard_map/all_to_all | solution.py:118

commit v2 on v1

--- a/solution.py
+++ b/solution.py
@@ -1,6 +1,8 @@
 import jax
 import jax.numpy as jnp
 from jax import lax
+from jax.experimental import pallas as pl
+from jax.experimental.pallas import tpu as pltpu
 from jax.sharding import PartitionSpec as P
 
 
@@ -55,6 +57,103 @@
     rank = jnp.dot(routed, before, preferred_element_type=jnp.float32)
     slot = jnp.where(routed > 0, rank, -1.0).astype(jnp.int32)
     return slot, row_weight
+
+
+GATE_CHUNKS = 8
+DOWN_CHUNKS = 8
+
+
+def experts_kernel(
+    rows_ref, gain_ref, gate_hbm, up_hbm, down_hbm, out_ref,
+    gate_ref, up_ref, down_ref, normed_ref, gate_sum, up_sum, act_ref, gate_sem, up_sem, down_sem,
+):
+    replicas, pieces, slots, chunk = rows_ref.shape
+    total = replicas * slots
+    width = pieces * chunk
+    depth = width // GATE_CHUNKS
+    span = width // DOWN_CHUNKS
+
+    def gate_copies(i):
+        rows = pl.ds(i * depth, depth)
+        return (
+            pltpu.make_async_copy(gate_hbm.at[rows, :], gate_ref.at[rows, :], gate_sem.at[i]),
+            pltpu.make_async_copy(up_hbm.at[rows, :], up_ref.at[rows, :], up_sem.at[i]),
+        )
+
+    def down_copy(i):
+        columns = pl.ds(i * span, span)
+        return pltpu.make_async_copy(
+            down_hbm.at[:, columns], down_ref.at[:, columns], down_sem.at[i]
+        )
+
+    for i in range(GATE_CHUNKS):
+        for copy in gate_copies(i):
+            copy.start()
+    for i in range(DOWN_CHUNKS):
+        down_copy(i).start()
+
+    squares = jnp.zeros((total, chunk), jnp.float32)
+    for piece in range(pieces):
+        part = rows_ref[:, piece].reshape(total, chunk).astype(jnp.float32)
+        squares = squares + part * part
+    spread = jnp.sum(squares, axis=-1, keepdims=True) * (1.0 / width)
+    scale = lax.rsqrt(spread + 1e-06)
+    for piece in range(pieces):
+        part = rows_ref[:, piece].reshape(total, chunk).astype(jnp.float32)
+        columns = pl.ds(piece * chunk, chunk)
+        normed_ref[:, columns] = (part * scale * gain_ref[:, columns]).astype(jnp.bfloat16)
+
+    for i in range(GATE_CHUNKS):
+        rows = pl.ds(i * depth, depth)
+        for copy in gate_copies(i):
+            copy.wait()
+        part = normed_ref[:, rows]
+        gate_part = jnp.dot(part, gate_ref[rows, :], preferred_element_type=jnp.float32)
+        up_part = jnp.dot(part, up_ref[rows, :], preferred_element_type=jnp.float32)
+        if i == 0:
+            gate_sum[...] = gate_part
+            up_sum[...] = up_part
+        else:
+            gate_sum[...] += gate_part
+            up_sum[...] += up_part
+    gates = gate_sum[...]
+    act_ref[...] = (gates / (1.0 + jnp.exp(-gates)) * up_sum[...]).astype(jnp.bfloat16)
+
+    per_copy = span // chunk
+    for piece in range(pieces):
+        if piece % per_copy == 0:
+            down_copy(piece // per_copy).wait()
+        columns = pl.ds(piece * chunk, chunk)
+        part = jnp.dot(act_ref[...], down_ref[:, columns], preferred_element_type=jnp.float32)
+        out_ref[:, piece] = part.astype(jnp.bfloat16).reshape(replicas, slots, chunk)
+
+
+def run_experts(rows, norm_gain, w_gate, w_up, w_down):
+    replicas, pieces, slots, chunk = rows.shape
+    width, hidden_units = w_gate.shape
+    total = replicas * slots
+    whole = pl.BlockSpec(memory_space=pltpu.VMEM)
+    left = pl.BlockSpec(memory_space=pl.ANY)
+    return pl.pallas_call(
+        experts_kernel,
+        out_shape=jax.ShapeDtypeStruct(rows.shape, jnp.bfloat16),
+        in_specs=[whole, whole, left, left, left],
+        out_specs=whole,
+        scratch_shapes=[
+            pltpu.VMEM((width, hidden_units), jnp.bfloat16),
+            pltpu.VMEM((width, hidden_units), jnp.bfloat16),
+            pltpu.VMEM((hidden_units, width), jnp.bfloat16),
+            pltpu.VMEM((total, width), jnp.bfloat16),
+            pltpu.VMEM((total, hidden_units), jnp.float32),
+            pltpu.VMEM((total, hidden_units), jnp.float32),
+            pltpu.VMEM((total, hidden_units), jnp.bfloat16),
+            pltpu.SemaphoreType.DMA((GATE_CHUNKS,)),
+            pltpu.SemaphoreType.DMA((GATE_CHUNKS,)),
+            pltpu.SemaphoreType.DMA((DOWN_CHUNKS,)),
+        ],
+        compiler_params=pltpu.CompilerParams(vmem_limit_bytes=48 * 1024 * 1024),
+        name="experts",
+    )(rows, norm_gain.reshape(1, width), w_gate, w_up, w_down)
 
 
 def shards(
@@ -105,16 +204,8 @@
     received = lax.all_to_all(outgoing, both, split_axis=0, concat_axis=0, tiled=True)
 
     rows = received.reshape(replica_count, tensor_width, cap_slots, chunk)
-    rows = rows.transpose(0, 2, 1, 3).reshape(replica_count * cap_slots, width)
-    widened = rows.astype(jnp.float32)
-    spread = jnp.mean(widened * widened, axis=-1, keepdims=True)
-    normed = (widened * lax.rsqrt(spread + 1e-06) * norm_gain).astype(jnp.bfloat16)
-    gate_part = jnp.dot(normed, w_gate[0], preferred_element_type=jnp.float32)
-    up_part = jnp.dot(normed, w_up[0], preferred_element_type=jnp.float32)
-    act = (jax.nn.silu(gate_part) * up_part).astype(jnp.bfloat16)
-    result = jnp.dot(act, w_down[0], preferred_element_type=jnp.float32).astype(jnp.bfloat16)
-    result = result.reshape(replica_count, cap_slots, tensor_width, chunk).transpose(0, 2, 1, 3)
-    answered = result.reshape(experts_all, cap_slots, chunk)
+    answered = run_experts(rows, norm_gain, w_gate[0], w_up[0], w_down[0])
+    answered = answered.reshape(experts_all, cap_slots, chunk)
     returned = lax.all_to_all(answered, both, split_axis=0, concat_axis=0, tiled=True)
 
     spread_weight = jnp.where(chosen, row_weight[:, None, :], 0.0)

time: 124 us -> 117 us (0.944)
  blocking collectives: 10.9 us -> 37 us
  waiting for transfers between devices: 54.3 us -> 35.4 us
  matrix products: 25.2 us -> 14.4 us
  Pallas kernels: 0 us -> 10 us
  starting transfers between devices: 19.4 us -> 11.9 us
  local copies, waits for them, and re-layouts: 6.38 us -> 3.18 us
  other arithmetic: 6.64 us -> 3.87 us
    all_to_all x0 -> x1, blocking collectives: none -> 26.1 us  [shards(): lax.all_to_all(outgoing, both, split_axis=0, concat_axis=0, tiled=True)]
    all_to_all x1 -> x0, waiting for transfers between devices: 18.8 us -> none  [shards(): lax.all_to_all(outgoing, both, split_axis=0, concat_axis=0, tiled=True)]
    dot_general x2 -> x0, matrix products: 10.8 us -> none  [the longest x1 7.06 us: shards(): jnp.dot(act, w_down[0], preferred_element_type=jnp.float32)]
    pallas_call x0 -> x1, Pallas kernels: none -> 10 us  [run_experts(): pl.pallas_call(experts_kernel, out_shape=jax.ShapeDtypeStruct(rows.shape,...]
    all_to_all x1 -> x0, starting transfers between devices: 7.48 us -> none  [shards(): lax.all_to_all(outgoing, both, split_axis=0, concat_axis=0, tiled=True)]
    convert_element_type x2 -> x0, other arithmetic: 1.47 us -> none  [the longest x1 1.19 us: shards(): (widened * lax.rsqrt(spread + 1e-06) * norm_gain).astype(jnp.bfloat16)]
    transpose x2 -> x0, local copies, waits for them, and re-layouts: 1.44 us -> none  [shards(): result.reshape(replica_count, cap_slots, tensor_width, chunk)]
    reduce_sum x1 -> x0, other arithmetic: 1.29 us -> none  [shards(): spread = jnp.mean(widened * widened, axis=-1, keepdims=True)]
  transfers between devices with their start and end apart: 3 -> 2, of which waited for: 3 -> 2; matrix products, arithmetic and copies ran while one was open for 1% -> 1% of each run, Pallas kernels for 0% -> 0%
where the time goes in v2:
time: 117 us; the launch traced here: 116 us
  blocking collectives  37 us (32%)
  waiting for transfers between devices  35.4 us (30%)
  matrix products  14.4 us (12%)
  starting transfers between devices  11.9 us (10%)
  Pallas kernels  10 us (9%)
  other arithmetic  3.87 us (3%)
  local copies, waits for them, and re-layouts  3.18 us (3%)
    all_to_all x1, blocking collectives, shards(): lax.all_to_all(outgoing, both, split_axis=0, concat_axis=0, tiled=True)  26.1 us
    all_to_all x1, waiting for transfers between devices, shards(): lax.all_to_all(answered, both, split_axis=0, concat_axis=0, tiled=True)  18.6 us
    all_to_all x1, waiting for transfers between devices, shards(): lax.all_to_all(partial, 'tensor', split_axis=0, concat_axis=0, tiled=True)  16.9 us
    all_to_all x1, blocking collectives, shards(): lax.all_to_all(layer.reshape(tensor_width, row_count // tensor_width, chu...  10.9 us
    pallas_call x1, Pallas kernels, run_experts(): pl.pallas_call(experts_kernel, out_shape=jax.ShapeDtypeStruct(rows.shape,...  10 us
    all_to_all x1, starting transfers between devices, shards(): lax.all_to_all(partial, 'tensor', split_axis=0, concat_axis=0, tiled=True)  7.25 us
    all_to_all x1, starting transfers between devices, shards(): lax.all_to_all(answered, both, split_axis=0, concat_axis=0, tiled=True)  4.65 us
    dot_general x1, matrix products, attend(): jnp.einsum('rhd,rpd->rhp', query_rows, cached_keys, preferred_element_typ...  4.56 us
  transfers between devices with their start and end apart: 2, of which 2 were waited for; matrix products, arithmetic and copies ran while one was open for 1% of the time, Pallas kernels for 0%

profile of v2, /device:TPU:0, one launch (start us, length us, event | category | flops | bytes accessed | tf_op | source)
XLA Modules:
  0.0 116.1 jit_solution(8735857916252307420)
XLA Ops:
  0.0 0.7 iota_compare_fusion.4
  0.7 1.1 dynamic-slice_convert_fusion
  1.9 0.9 reshape.47
  2.8 0.3 fusion.46
  3.1 4.6 %fusion.53 = (f32[128,4]{1,0:T(8,128)S(1)}, f32[128,4,128]{2,1,0:T(4,128)S(1)}) fusion(bf16[128,4,128]{2,1,0:T(4,128)(2,1)S(1)} %reshape.47, bf16[128,1,128,128]{3,2,1,0:T(8,128)(2,1)} %param.18, pred[128,128]{1,0:T(8,128)(4,1)S(1)} %iota_compare_fusion.4), kind=kOutput, calls=%fused_computation.62 | convolution fusion | flops 16973312 | bytes 4605952 | tf_op jit(solution)/shard_map/rhd,rpd->rhp/dot_general | solution.py:21
  7.9 0.4 fusion.42
  8.6 3.4 %fusion.22 = bf16[128,4,128]{2,1,0:T(4,128)(2,1)S(1)} fusion(bf16[128,1,128,128]{3,2,1,0:T(8,128)(2,1)} %param.19, f32[128,4,128]{2,1,0:T(4,128)S(1)} %get-tuple-element.8, f32[128,128]{1,0:T(8,128)S(1)} %bitcast.88, f32[128,4]{1,0:T(8,128)S(1)} %copy.67, f32[128,4]{1,0:T(8,128)S(1)} %copy.66, f32[128,4]{1,0:T(8,128)S(1)} %copy.64), kind=kOutput, calls=%fused_computation.16 | convolution fusion | flops 17170432 | bytes 4659200 | tf_op jit(solution)/shard_map/rhp,rpd->rhd/dot_general | solution.py:38
  12.2 4.0 %fusion.10 = bf16[16,128,256]{2,1,0:T(8,128)(2,1)} fusion(bf16[128,512,1]{1,0,2:T(8,128)(2,1)S(1)} %reshape.58, bf16[64,16,8,256]{3,2,1,0:T(8,128)(2,1)} %bitcast.90), kind=kOutput, calls=%fused_computation.12 | convolution fusion | flops 537395200 | bytes 5373952 | tf_op jit(solution)/shard_map/rk,ktj->trj/dot_general | solution.py:187
  16.1 7.2 %all-to-all-start = ((bf16[16,128,256]{2,1,0:T(8,128)(2,1)}), bf16[16,128,256]{2,1,0:T(8,128)(2,1)S(1)}, u32[]{:S(2)}, u32[]{:S(2)}) async-start(bf16[16,128,256]{2,1,0:T(8,128)(2,1)} %fusion.10), calls=%async_computation | async-start | bytes 2097152 | tf_op jit(solution)/shard_map/all_to_all | solution.py:193
  23.5 0.3 fusion.41
  23.9 0.2 fusion.29
  24.2 16.9 %all-to-all-done = bf16[16,128,256]{2,1,0:T(8,128)(2,1)S(1)} async-done(((bf16[16,128,256]{2,1,0:T(8,128)(2,1)}), bf16[16,128,256]{2,1,0:T(8,128)(2,1)S(1)}, u32[]{:S(2)}, u32[]{:S(2)}) %all-to-all-start) | async-done | bytes 1048608 | tf_op jit(solution)/shard_map/all_to_all | solution.py:193
  41.2 0.9 add_convert_fusion
  42.1 0.5 convolution_convert_fusion
  42.6 0.6 copy.74
  43.2 26.1 %all_to_all.20 = bf16[128,16,256]{2,1,0:T(8,128)(2,1)S(1)} all-to-all(bf16[128,16,256]{2,1,0:T(8,128)(2,1)S(1)} %copy.74), channel_id=1, replica_groups=mesh['dp'=8,'tensor'=16] {'dp','tensor'}, dimensions={0} | all-to-all | bytes 2097152 | tf_op jit(solution)/shard_map/all_to_all | solution.py:204
  69.3 10.0 %experts.1 = bf16[8,16,16,256]{3,2,1,0:T(8,128)(2,1)} custom-call(bf16[8,16,16,256]{3,2,1,0:T(8,128)(2,1)S(1)} %bitcast.80, f32[1,4096]{1,0:T(1,128)S(1)} %bitcast.81, bf16[4096,768]{1,0:T(8,128)(2,1)} %bitcast.82, bf16[4096,768]{1,0:T(8,128)(2,1)} %bitcast.83, bf16[768,4096]{1,0:T(8,128)(2,1)} %bitcast.84), custom_call_target="tpu_custom_call" | custom-call | tf_op jit(solution)/shard_map/experts/pallas_call | solution.py:137
  79.4 4.6 %all-to-all-start.2 = ((bf16[128,16,256]{2,1,0:T(8,128)(2,1)}), bf16[128,16,256]{2,1,0:T(8,128)(2,1)S(1)}, u32[]{:S(2)}, u32[]{:S(2)}) async-start(bf16[128,16,256]{2,1,0:T(8,128)(2,1)} %bitcast.15), calls=%async_computation.2 | async-start | bytes 2097152 | tf_op jit(solution)/shard_map/all_to_all | solution.py:209
  84.1 0.3 select_reduce_fusion
  84.5 18.6 %all-to-all-done.2 = bf16[128,16,256]{2,1,0:T(8,128)(2,1)S(1)} async-done(((bf16[128,16,256]{2,1,0:T(8,128)(2,1)}), bf16[128,16,256]{2,1,0:T(8,128)(2,1)S(1)}, u32[]{:S(2)}, u32[]{:S(2)}) %all-to-all-start.2) | async-done | bytes 1048608 | tf_op jit(solution)/shard_map/all_to_all | solution.py:209
  103.1 0.8 convolution_bitcast_fusion
  103.8 0.7 fusion.28
  104.6 10.9 %all_to_all.21 = bf16[16,8,256]{2,1,0:T(8,128)(2,1)S(1)} all-to-all(bf16[16,8,256]{2,1,0:T(8,128)(2,1)S(1)} %fusion.28), channel_id=1, replica_groups=mesh['dp'=8,'tensor'=16] {'tensor'}, dimensions={0} | all-to-all | bytes 131072 | tf_op jit(solution)/shard_map/all_to_all | solution.py:218
  115.4 0.6 copy.99
  (23 shorter events, 1.2 us)
Async XLA Ops:
  12.1 11.3 %copy-start.2 = (s32[128,8]{0,1:T(8,128)S(1)}, s32[128,8]{0,1:T(8,128)}, u32[]{:S(2)}) copy-start(s32[128,8]{0,1:T(8,128)} %param.23) | copy-start | bytes 12292
  16.1 53.2 %copy-start = (f32[4096]{0:T(1024)S(1)}, f32[4096]{0:T(1024)}, u32[]{:S(2)}) copy-start(f32[4096]{0:T(1024)} %param.22) | copy-start | bytes 49156
  16.1 25.0 %all-to-all-start = ((bf16[16,128,256]{2,1,0:T(8,128)(2,1)}), bf16[16,128,256]{2,1,0:T(8,128)(2,1)S(1)}, u32[]{:S(2)}, u32[]{:S(2)}) async-start(bf16[16,128,256]{2,1,0:T(8,128)(2,1)} %fusion.10), calls=%async_computation | async-start | bytes 2097152 | tf_op jit(solution)/shard_map/all_to_all | solution.py:193
  69.3 14.7 %copy-start.1 = (f32[128,8]{0,1:T(8,128)S(1)}, f32[128,8]{0,1:T(8,128)}, u32[]{:S(2)}) copy-start(f32[128,8]{0,1:T(8,128)} %param.24) | copy-start | bytes 12292
  79.4 23.7 %all-to-all-start.2 = ((bf16[128,16,256]{2,1,0:T(8,128)(2,1)}), bf16[128,16,256]{2,1,0:T(8,128)(2,1)S(1)}, u32[]{:S(2)}, u32[]{:S(2)}) async-start(bf16[128,16,256]{2,1,0:T(8,128)(2,1)} %bitcast.15), calls=%async_computation.2 | async-start | bytes 2097152 | tf_op jit(solution)/shard_map/all_to_all | solution.py:209

commit v3 on v2

v3 whole, which is shorter than its diff:
```python
import jax
import jax.numpy as jnp
from jax import lax
from jax.experimental import pallas as pl
from jax.experimental.pallas import tpu as pltpu
from jax.sharding import PartitionSpec as P


ROWS_STEP = 32
STEPS_AHEAD = 3
WEIGHT_COPIES = 4


def attend_kernel(
    head_ref, lengths_hbm, query_hbm, fresh_key_hbm, fresh_value_hbm, key_hbm, value_hbm, weight_hbm,
    out_ref,
    lengths_ref, query_ref, fresh_key_ref, fresh_value_ref, key_ref, value_ref, weight_ref,
    query_scr, own_key_scr, own_value_scr, attended_scr, heads_scr,
    small_sem, key_sem, value_sem, weight_sem,
):
    row_count, positions, head_size = key_ref.shape
    head_count = query_ref.shape[1] // head_size
    pieces, _, chunk = out_ref.shape
    steps = row_count // ROWS_STEP
    width = weight_ref.shape[0] // WEIGHT_COPIES
    score_scale = head_size ** (-0.5)

    def cache_copies(step):
        rows = pl.ds(step * ROWS_STEP, ROWS_STEP)
        return (
            pltpu.make_async_copy(key_hbm.at[rows], key_ref.at[rows], key_sem.at[step]),
            pltpu.make_async_copy(value_hbm.at[rows], value_ref.at[rows], value_sem.at[step]),
        )

    def weight_copy(i):
        rows = pl.ds(i * width, width)
        return pltpu.make_async_copy(weight_hbm.at[rows], weight_ref.at[rows], weight_sem.at[i])

    small = [
        pltpu.make_async_copy(query_hbm, query_ref, small_sem.at[0]),
        pltpu.make_async_copy(fresh_key_hbm, fresh_key_ref, small_sem.at[1]),
        pltpu.make_async_copy(fresh_value_hbm, fresh_value_ref, small_sem.at[2]),
        pltpu.make_async_copy(lengths_hbm, lengths_ref, small_sem.at[3]),
    ]
    for copy in small:
        copy.start()
    for step in range(STEPS_AHEAD):
        for copy in cache_copies(step):
            copy.start()
    for copy in small:
        copy.wait()

    group = lax.broadcasted_iota(jnp.int32, fresh_key_ref.shape, 1) == head_ref[0]
    own_key = jnp.sum(jnp.where(group, fresh_key_ref[...].astype(jnp.float32), 0.0), axis=1)
    own_value = jnp.sum(jnp.where(group, fresh_value_ref[...].astype(jnp.float32), 0.0), axis=1)
    for head in range(head_count):
        rows = pl.ds(head, row_count, stride=head_count)
        columns = pl.ds(head * head_size, head_size)
        query_scr[rows, :] = query_ref[:, columns].astype(jnp.float32)
        own_key_scr[rows, :] = own_key
        own_value_scr[rows, :] = own_value

    pair = 2 * head_count
    upper = lax.broadcasted_iota(jnp.int32, (pair, positions), 0) < head_count
    position = lax.broadcasted_iota(jnp.int32, (pair, positions), 1)

    @pl.loop(0, steps)
    def _(step):
        for copy in cache_copies(step):
            copy.wait()

        @pl.when(step + STEPS_AHEAD < steps)
        def _():
            for copy in cache_copies(step + STEPS_AHEAD):
                copy.start()

        @pl.when(step + WEIGHT_COPIES >= steps)
        def _():
            weight_copy(step + WEIGHT_COPIES - steps).start()

        first = pl.multiple_of(step * (ROWS_STEP * head_count), ROWS_STEP * head_count)
        queries = query_scr[pl.ds(first, ROWS_STEP * head_count), :]
        parts = []
        for i in range(ROWS_STEP // 2):
            row = step * ROWS_STEP + 2 * i
            keys = key_ref[pl.ds(row, 2)].reshape(2 * positions, head_size)
            asked = queries[i * pair : (i + 1) * pair].astype(jnp.bfloat16)
            both = lax.dot_general(
                asked, keys, (((1,), (1,)), ((), ())), preferred_element_type=jnp.float32
            )
            scores = jnp.where(upper, both[:, :positions], both[:, positions:]) * score_scale
            live = jnp.where(upper, lengths_ref[row], lengths_ref[row + 1])
            parts.append(jnp.where(position < live, scores, -1e30))
        scores = jnp.concatenate(parts, axis=0)
        own_keys = own_key_scr[pl.ds(first, ROWS_STEP * head_count), :]
        own_score = jnp.sum(queries * own_keys, axis=-1, keepdims=True) * score_scale
        row_max = jnp.maximum(jnp.max(scores, axis=-1, keepdims=True), own_score)
        terms = jnp.exp(scores - row_max)
        own_term = jnp.exp(own_score - row_max)
        total = jnp.sum(terms, axis=-1, keepdims=True) + own_term
        probs = (terms / total).astype(jnp.bfloat16).astype(jnp.float32)
        own_prob = (own_term / total).astype(jnp.bfloat16).astype(jnp.float32)
        parts = []
        for i in range(ROWS_STEP // 2):
            row = step * ROWS_STEP + 2 * i
            values = value_ref[pl.ds(row, 2)].reshape(2 * positions, head_size)
            prob = probs[i * pair : (i + 1) * pair]
            spread = jnp.concatenate(
                [jnp.where(upper, prob, 0.0), jnp.where(upper, 0.0, prob)], axis=1
            ).astype(jnp.bfloat16)
            parts.append(jnp.dot(spread, values, preferred_element_type=jnp.float32))
        attended = jnp.concatenate(parts, axis=0)
        own_values = own_value_scr[pl.ds(first, ROWS_STEP * head_count), :]
        attended_scr[pl.ds(first, ROWS_STEP * head_count), :] = attended + own_prob * own_values

    for head in range(head_count):
        columns = pl.ds(head * head_size, head_size)
        rows = pl.ds(head, row_count, stride=head_count)
        heads_scr[:, columns] = attended_scr[rows, :].astype(jnp.bfloat16)
    for i in range(WEIGHT_COPIES):
        weight_copy(i).wait()
    for piece in range(pieces):
        columns = pl.ds(piece * chunk, chunk)
        part = jnp.dot(
            heads_scr[...], weight_ref[:, columns], preferred_element_type=jnp.float32
        )
        out_ref[piece] = part.astype(jnp.bfloat16)


def run_attend(query, fresh_key, fresh_value, key_cache, value_cache, lengths, kv_head, out_weight, pieces):
    row_count, positions, head_size = key_cache.shape
    width = out_weight.shape[1]
    many = query.shape[0] * query.shape[1] // head_size
    whole = pl.BlockSpec(memory_space=pltpu.VMEM)
    scalars = pl.BlockSpec(memory_space=pltpu.SMEM)
    left = pl.BlockSpec(memory_space=pltpu.HBM)
    steps = row_count // ROWS_STEP
    return pl.pallas_call(
        attend_kernel,
        out_shape=jax.ShapeDtypeStruct((pieces, row_count, width // pieces), jnp.bfloat16),
        in_specs=[scalars] + [left] * 7,
        out_specs=whole,
        scratch_shapes=[
            pltpu.SMEM(lengths.shape, jnp.int32),
            pltpu.VMEM(query.shape, jnp.bfloat16),
            pltpu.VMEM(fresh_key.shape, jnp.bfloat16),
            pltpu.VMEM(fresh_value.shape, jnp.bfloat16),
            pltpu.VMEM(key_cache.shape, jnp.bfloat16),
            pltpu.VMEM(value_cache.shape, jnp.bfloat16),
            pltpu.VMEM(out_weight.shape, jnp.bfloat16),
            pltpu.VMEM((many, head_size), jnp.float32),
            pltpu.VMEM((many, head_size), jnp.float32),
            pltpu.VMEM((many, head_size), jnp.float32),
            pltpu.VMEM((many, head_size), jnp.float32),
            pltpu.VMEM(query.shape, jnp.bfloat16),
            pltpu.SemaphoreType.DMA((4,)),
            pltpu.SemaphoreType.DMA((steps,)),
            pltpu.SemaphoreType.DMA((steps,)),
            pltpu.SemaphoreType.DMA((WEIGHT_COPIES,)),
        ],
        compiler_params=pltpu.CompilerParams(vmem_limit_bytes=60 * 1024 * 1024),
        name="attend",
    )(kv_head, lengths, query, fresh_key, fresh_value, key_cache, value_cache, out_weight)


def route(expert_ids, gate_scores, experts_all):
    row_count = expert_ids.shape[0]
    expert_axis = lax.broadcasted_iota(jnp.int32, (1, 1, experts_all), 2)
    matches = expert_ids[:, :, None] == expert_axis
    weights = gate_scores / jnp.sum(gate_scores, axis=1, keepdims=True)
    row_weight = jnp.sum(jnp.where(matches, weights[:, :, None], 0.0), axis=1).T
    routed = jnp.any(matches, axis=1).astype(jnp.bfloat16).T
    before = (
        lax.broadcasted_iota(jnp.int32, (row_count, row_count), 0)
        < lax.broadcasted_iota(jnp.int32, (row_count, row_count), 1)
    ).astype(jnp.bfloat16)
    rank = jnp.dot(routed, before, preferred_element_type=jnp.float32)
    slot = jnp.where(routed > 0, rank, -1.0).astype(jnp.int32)
    return slot, row_weight


UNIT_CHUNK = 256
DOWN_CHUNKS = 4
COPIES_AHEAD = 6


def experts_kernel(
    rows_ref, gain_ref, gate_hbm, up_hbm, down_hbm, out_ref,
    gate_ref, up_ref, down_ref, normed_ref, act_ref, gate_sem, up_sem, down_sem,
):
    replicas, pieces, slots, chunk = rows_ref.shape
    total = replicas * slots
    width = pieces * chunk
    unit_chunks = gate_ref.shape[1] // UNIT_CHUNK
    span = width // DOWN_CHUNKS

    def unit_copies(i):
        units = pl.ds(i * UNIT_CHUNK, UNIT_CHUNK)
        return (
            pltpu.make_async_copy(gate_hbm.at[:, units], gate_ref.at[:, units], gate_sem.at[i]),
            pltpu.make_async_copy(up_hbm.at[:, units], up_ref.at[:, units], up_sem.at[i]),
        )

    def down_copy(i):
        columns = pl.ds(i * span, span)
        return pltpu.make_async_copy(
            down_hbm.at[:, columns], down_ref.at[:, columns], down_sem.at[i]
        )

    order = [copy for i in range(unit_chunks) for copy in unit_copies(i)]
    order += [down_copy(i) for i in range(DOWN_CHUNKS)]
    for copy in order[:COPIES_AHEAD]:
        copy.start()

    def take(i):
        order[i].wait()
        if i + COPIES_AHEAD < len(order):
            order[i + COPIES_AHEAD].start()

    squares = jnp.zeros((total, chunk), jnp.float32)
    for piece in range(pieces):
        part = rows_ref[:, piece].reshape(total, chunk).astype(jnp.float32)
        squares = squares + part * part
    spread = jnp.sum(squares, axis=-1, keepdims=True) * (1.0 / width)
    scale = lax.rsqrt(spread + 1e-06)
    for piece in range(pieces):
        part = rows_ref[:, piece].reshape(total, chunk).astype(jnp.float32)
        columns = pl.ds(piece * chunk, chunk)
        normed_ref[:, columns] = (part * scale * gain_ref[:, columns]).astype(jnp.bfloat16)

    for i in range(unit_chunks):
        units = pl.ds(i * UNIT_CHUNK, UNIT_CHUNK)
        take(2 * i)
        gates = jnp.dot(normed_ref[...], gate_ref[:, units], preferred_element_type=jnp.float32)
        take(2 * i + 1)
        ups = jnp.dot(normed_ref[...], up_ref[:, units], preferred_element_type=jnp.float32)
        act_ref[:, units] = (gates / (1.0 + jnp.exp(-gates)) * ups).astype(jnp.bfloat16)

    per_copy = span // chunk
    for piece in range(pieces):
        if piece % per_copy == 0:
            take(2 * unit_chunks + piece // per_copy)
        columns = pl.ds(piece * chunk, chunk)
        part = jnp.dot(act_ref[...], down_ref[:, columns], preferred_element_type=jnp.float32)
        out_ref[:, piece] = part.astype(jnp.bfloat16).reshape(replicas, slots, chunk)


def run_experts(rows, norm_gain, w_gate, w_up, w_down):
    replicas, pieces, slots, chunk = rows.shape
    width, hidden_units = w_gate.shape
    total = replicas * slots
    unit_chunks = hidden_units // UNIT_CHUNK
    whole = pl.BlockSpec(memory_space=pltpu.VMEM)
    left = pl.BlockSpec(memory_space=pltpu.HBM)
    return pl.pallas_call(
        experts_kernel,
        out_shape=jax.ShapeDtypeStruct(rows.shape, jnp.bfloat16),
        in_specs=[whole, whole, left, left, left],
        out_specs=whole,
        scratch_shapes=[
            pltpu.VMEM((width, hidden_units), jnp.bfloat16),
            pltpu.VMEM((width, hidden_units), jnp.bfloat16),
            pltpu.VMEM((hidden_units, width), jnp.bfloat16),
            pltpu.VMEM((total, width), jnp.bfloat16),
            pltpu.VMEM((total, hidden_units), jnp.bfloat16),
            pltpu.SemaphoreType.DMA((unit_chunks,)),
            pltpu.SemaphoreType.DMA((unit_chunks,)),
            pltpu.SemaphoreType.DMA((DOWN_CHUNKS,)),
        ],
        compiler_params=pltpu.CompilerParams(vmem_limit_bytes=60 * 1024 * 1024),
        name="experts",
    )(rows, norm_gain.reshape(1, width), w_gate, w_up, w_down)


def shards(
    residual_in,
    query,
    fresh_key,
    fresh_value,
    key_cache,
    value_cache,
    lengths,
    out_weight,
    norm_gain,
    expert_ids,
    gate_scores,
    w_gate,
    w_up,
    w_down,
):
    both = ("dp", "tensor")
    row_count, width = residual_in.shape
    tensor_width = lax.axis_size("tensor")
    replica_count = lax.axis_size("dp")
    experts_all = replica_count * tensor_width
    column = lax.axis_index("tensor")
    chunk = width // tensor_width
    cap_slots = 2 * max(1, row_count * expert_ids.shape[1] // experts_all)

    kv_head = (column // (tensor_width // fresh_key.shape[1])).astype(jnp.int32).reshape(1)
    partial = run_attend(
        query, fresh_key, fresh_value, key_cache[:, 0], value_cache[:, 0], lengths, kv_head,
        out_weight, tensor_width,
    )
    pieces = lax.all_to_all(partial, "tensor", split_axis=0, concat_axis=0, tiled=True)
    proj = jnp.sum(pieces.astype(jnp.float32), axis=0)
    residual = lax.dynamic_slice_in_dim(residual_in, column * chunk, chunk, 1)
    hidden = (residual.astype(jnp.float32) + proj).astype(jnp.bfloat16)

    slot, row_weight = route(expert_ids, gate_scores, experts_all)
    slot_axis = lax.broadcasted_iota(jnp.int32, (1, cap_slots, 1), 1)
    chosen = slot[:, None, :] == slot_axis
    outgoing = jnp.einsum(
        "esr,rj->esj", chosen.astype(jnp.bfloat16), hidden, preferred_element_type=jnp.float32
    ).astype(jnp.bfloat16)
    received = lax.all_to_all(outgoing, both, split_axis=0, concat_axis=0, tiled=True)

    rows = received.reshape(replica_count, tensor_width, cap_slots, chunk)
    answered = run_experts(rows, norm_gain, w_gate[0], w_up[0], w_down[0])
    answered = answered.reshape(experts_all, cap_slots, chunk)
    returned = lax.all_to_all(answered, both, split_axis=0, concat_axis=0, tiled=True)

    spread_weight = jnp.where(chosen, row_weight[:, None, :], 0.0)
    coarse = spread_weight.astype(jnp.bfloat16)
    fine = (spread_weight - coarse.astype(jnp.float32)).astype(jnp.bfloat16)
    mixture = jnp.einsum(
        "esr,esj->rj", coarse, returned, preferred_element_type=jnp.float32
    ) + jnp.einsum("esr,esj->rj", fine, returned, preferred_element_type=jnp.float32)
    layer = (hidden.astype(jnp.float32) + mixture).astype(jnp.bfloat16)
    own = lax.all_to_all(
        layer.reshape(tensor_width, row_count // tensor_width, chunk),
        "tensor",
        split_axis=0,
        concat_axis=0,
        tiled=True,
    )
    return own.transpose(1, 0, 2).reshape(row_count // tensor_width, width)


def solution(mesh):
    placed = (
        P("dp", None),
        P("dp", "tensor"),
        P("dp", None, None),
        P("dp", None, None),
        P("dp", "tensor", None, None),
        P("dp", "tensor", None, None),
        P("dp"),
        P("tensor", None),
        P(),
        P("dp", None),
        P("dp", None),
        P(("dp", "tensor"), None, None),
        P(("dp", "tensor"), None, None),
        P(("dp", "tensor"), None, None),
    )
    return jax.shard_map(
        shards, mesh=mesh, in_specs=placed, out_specs=P(("dp", "tensor"), None), check_vma=False
    )
```

time: 117 us -> 108 us (0.923)
  matrix products: 14.4 us -> 2.2 us
  Pallas kernels: 10 us -> 17.4 us
  other arithmetic: 3.87 us -> 1.63 us
  local copies, waits for them, and re-layouts: 3.18 us -> 1.62 us
    dot_general x4 -> x0, matrix products: 12.2 us -> none  [the longest x1 4.56 us: attend(): jnp.einsum('rhd,rpd->rhp', query_rows, cached_keys, preferred_element_typ...]
    pallas_call x0 -> x1, Pallas kernels: none -> 7.8 us  [run_attend(): pl.pallas_call(attend_kernel, out_shape=jax.ShapeDtypeStruct((pieces, row...]
where the time goes in v3:
time: 108 us; the launch traced here: 107 us
  blocking collectives  37.1 us (34%)
  waiting for transfers between devices  35.4 us (33%)
  Pallas kernels  17.4 us (16%)
  starting transfers between devices  11.8 us (11%)
  matrix products  2.2 us (2%)
  other arithmetic  1.63 us (2%)
  local copies, waits for them, and re-layouts  1.62 us (2%)
    all_to_all x1, blocking collectives, shards(): lax.all_to_all(outgoing, both, split_axis=0, concat_axis=0, tiled=True)  26.3 us
    all_to_all x1, waiting for transfers between devices, shards(): lax.all_to_all(answered, both, split_axis=0, concat_axis=0, tiled=True)  18.6 us
    all_to_all x1, waiting for transfers between devices, shards(): lax.all_to_all(partial, 'tensor', split_axis=0, concat_axis=0, tiled=True)  16.9 us
    all_to_all x1, blocking collectives, shards(): lax.all_to_all(layer.reshape(tensor_width, row_count // tensor_width, chu...  10.9 us
    pallas_call x1, Pallas kernels, run_experts(): pl.pallas_call(experts_kernel, out_shape=jax.ShapeDtypeStruct(rows.shape,...  9.62 us
    pallas_call x1, Pallas kernels, run_attend(): pl.pallas_call(attend_kernel, out_shape=jax.ShapeDtypeStruct((pieces, row...  7.8 us
    all_to_all x1, starting transfers between devices, shards(): lax.all_to_all(partial, 'tensor', split_axis=0, concat_axis=0, tiled=True)  7.13 us
    all_to_all x1, starting transfers between devices, shards(): lax.all_to_all(answered, both, split_axis=0, concat_axis=0, tiled=True)  4.65 us
  transfers between devices with their start and end apart: 2, of which 2 were waited for; matrix products, arithmetic and copies ran while one was open for 1% of the time, Pallas kernels for 0%

profile of v3, /device:TPU:0, one launch (start us, length us, event | category | flops | bytes accessed | tf_op | source)
XLA Modules:
  0.0 107.3 jit_solution(8650000742899289203)
XLA Ops:
  0.0 7.8 %attend.1 = bf16[16,128,256]{2,1,0:T(8,128)(2,1)} custom-call(s32[1]{0:T(128)} %bitcast.head_ref, s32[128]{0:T(128)} %lengths_hbm.1, bf16[128,512]{1,0:T(8,128)(2,1)} %query_hbm.1, bf16[128,4,128]{2,1,0:T(4,128)(2,1)} %fresh_key_hbm.1, bf16[128,4,128]{2,1,0:T(4,128)(2,1)} %fresh_value_hbm.1, bf16[128,128,128]{2,1,0:T(8,128)(2,1)} %bitcast.38, ...), custom_call_target="tpu_custom_call" | custom-call | tf_op jit(solution)/shard_map/attend/pallas_call | solution.py:138
  7.8 7.1 %all-to-all-start = ((bf16[16,128,256]{2,1,0:T(8,128)(2,1)}), bf16[16,128,256]{2,1,0:T(8,128)(2,1)S(1)}, u32[]{:S(2)}, u32[]{:S(2)}) async-start(bf16[16,128,256]{2,1,0:T(8,128)(2,1)} %attend.1), calls=%async_computation | async-start | bytes 2097152 | tf_op jit(solution)/shard_map/all_to_all | solution.py:305
  14.9 0.0 copy-done.1
  15.0 0.1 copy.28
  15.1 0.3 fusion.16
  15.3 0.1 copy.29
  15.4 0.2 fusion.4
  15.7 0.1 copy.30
  15.8 16.9 %all-to-all-done = bf16[16,128,256]{2,1,0:T(8,128)(2,1)S(1)} async-done(((bf16[16,128,256]{2,1,0:T(8,128)(2,1)}), bf16[16,128,256]{2,1,0:T(8,128)(2,1)S(1)}, u32[]{:S(2)}, u32[]{:S(2)}) %all-to-all-start) | async-done | bytes 1048608 | tf_op jit(solution)/shard_map/all_to_all | solution.py:305
  32.7 0.1 convert_reduce_fusion
  32.8 0.9 add_convert_fusion
  33.7 0.5 convolution_convert_fusion
  34.2 0.6 copy.33
  34.7 26.3 %all_to_all.20 = bf16[128,16,256]{2,1,0:T(8,128)(2,1)} all-to-all(bf16[128,16,256]{2,1,0:T(8,128)(2,1)S(1)} %copy.33), channel_id=1, replica_groups=mesh['dp'=8,'tensor'=16] {'dp','tensor'}, dimensions={0} | all-to-all | bytes 2097152 | tf_op jit(solution)/shard_map/all_to_all | solution.py:316
  61.0 9.6 %experts.1 = bf16[8,16,16,256]{3,2,1,0:T(8,128)(2,1)} custom-call(bf16[8,16,16,256]{3,2,1,0:T(8,128)(2,1)} %bitcast.37, f32[1,4096]{1,0:T(1,128)} %bitcast.43, bf16[4096,768]{1,0:T(8,128)(2,1)} %bitcast.33, bf16[4096,768]{1,0:T(8,128)(2,1)} %bitcast.34, bf16[768,4096]{1,0:T(8,128)(2,1)} %bitcast.35), custom_call_target="tpu_custom_call" | custom-call | tf_op jit(solution)/shard_map/experts/pallas_call | solution.py:255
  70.6 4.6 %all-to-all-start.2 = ((bf16[128,16,256]{2,1,0:T(8,128)(2,1)}), bf16[128,16,256]{2,1,0:T(8,128)(2,1)S(1)}, u32[]{:S(2)}, u32[]{:S(2)}) async-start(bf16[128,16,256]{2,1,0:T(8,128)(2,1)} %bitcast.36), calls=%async_computation.2 | async-start | bytes 2097152 | tf_op jit(solution)/shard_map/all_to_all | solution.py:321
  75.3 0.0 copy-done
  75.3 0.1 copy.31
  75.4 0.3 select_reduce_fusion
  75.8 18.6 %all-to-all-done.2 = bf16[128,16,256]{2,1,0:T(8,128)(2,1)S(1)} async-done(((bf16[128,16,256]{2,1,0:T(8,128)(2,1)}), bf16[128,16,256]{2,1,0:T(8,128)(2,1)S(1)}, u32[]{:S(2)}, u32[]{:S(2)}) %all-to-all-start.2) | async-done | bytes 1048608 | tf_op jit(solution)/shard_map/all_to_all | solution.py:321
  94.3 0.8 convolution_bitcast_fusion
  95.1 0.7 fusion.3
  95.8 10.9 %all_to_all.21 = bf16[16,8,256]{2,1,0:T(8,128)(2,1)S(1)} all-to-all(bf16[16,8,256]{2,1,0:T(8,128)(2,1)S(1)} %fusion.3), channel_id=1, replica_groups=mesh['dp'=8,'tensor'=16] {'tensor'}, dimensions={0} | all-to-all | bytes 131072 | tf_op jit(solution)/shard_map/all_to_all | solution.py:330
  106.7 0.6 copy.42
  (4 shorter events, 0.0 us)
Async XLA Ops:
  0.0 15.0 %copy-start.1 = (s32[128,8]{0,1:T(8,128)S(1)}, s32[128,8]{0,1:T(8,128)}, u32[]{:S(2)}) copy-start(s32[128,8]{0,1:T(8,128)} %param.23) | copy-start | bytes 12292
  7.8 24.8 %all-to-all-start = ((bf16[16,128,256]{2,1,0:T(8,128)(2,1)}), bf16[16,128,256]{2,1,0:T(8,128)(2,1)S(1)}, u32[]{:S(2)}, u32[]{:S(2)}) async-start(bf16[16,128,256]{2,1,0:T(8,128)(2,1)} %attend.1), calls=%async_computation | async-start | bytes 2097152 | tf_op jit(solution)/shard_map/all_to_all | solution.py:305
  61.0 14.3 %copy-start = (f32[128,8]{0,1:T(8,128)S(1)}, f32[128,8]{0,1:T(8,128)}, u32[]{:S(2)}) copy-start(f32[128,8]{0,1:T(8,128)} %param.24) | copy-start | bytes 12292
  70.6 23.7 %all-to-all-start.2 = ((bf16[128,16,256]{2,1,0:T(8,128)(2,1)}), bf16[128,16,256]{2,1,0:T(8,128)(2,1)S(1)}, u32[]{:S(2)}, u32[]{:S(2)}) async-start(bf16[128,16,256]{2,1,0:T(8,128)(2,1)} %bitcast.36), calls=%async_computation.2 | async-start | bytes 2097152 | tf_op jit(solution)/shard_map/all_to_all | solution.py:321

commit v4 on v3

--- a/solution.py
+++ b/solution.py
@@ -163,60 +163,91 @@
     )(kv_head, lengths, query, fresh_key, fresh_value, key_cache, value_cache, out_weight)
 
 
-def route(expert_ids, gate_scores, experts_all):
+def route_kernel(column_ref, ids_ref, scores_ref, residual_hbm, slot_ref, weight_ref, residual_ref, sem):
+    experts, row_count = slot_ref.shape
+    chunk = residual_ref.shape[1]
+    own = pl.ds(pl.multiple_of(column_ref[0] * chunk, chunk), chunk)
+    copy = pltpu.make_async_copy(residual_hbm.at[:, own], residual_ref, sem)
+    copy.start()
+    topk = ids_ref.shape[0]
+    scores = scores_ref[...]
+    weights = scores / jnp.sum(scores, axis=0, keepdims=True)
+    expert = lax.broadcasted_iota(jnp.int32, (experts, row_count), 0)
+    named = jnp.zeros((experts, row_count), jnp.float32)
+    weight = jnp.zeros((experts, row_count), jnp.float32)
+    for k in range(topk):
+        match = ids_ref[k : k + 1, :] == expert
+        named = named + jnp.where(match, 1.0, 0.0)
+        weight = weight + jnp.where(match, weights[k : k + 1, :], 0.0)
+    earlier = lax.broadcasted_iota(jnp.int32, (row_count, row_count), 0)
+    later = lax.broadcasted_iota(jnp.int32, (row_count, row_count), 1)
+    before = jnp.where(earlier < later, 1.0, 0.0).astype(jnp.bfloat16)
+    rank = jnp.dot(named.astype(jnp.bfloat16), before, preferred_element_type=jnp.float32)
+    slot_ref[...] = jnp.where(named > 0.0, rank, -1.0).astype(jnp.int32)
+    weight_ref[...] = weight
+    copy.wait()
+
+
+def run_route(column, expert_ids, gate_scores, residual_in, experts_all, chunk):
     row_count = expert_ids.shape[0]
-    expert_axis = lax.broadcasted_iota(jnp.int32, (1, 1, experts_all), 2)
-    matches = expert_ids[:, :, None] == expert_axis
-    weights = gate_scores / jnp.sum(gate_scores, axis=1, keepdims=True)
-    row_weight = jnp.sum(jnp.where(matches, weights[:, :, None], 0.0), axis=1).T
-    routed = jnp.any(matches, axis=1).astype(jnp.bfloat16).T
-    before = (
-        lax.broadcasted_iota(jnp.int32, (row_count, row_count), 0)
-        < lax.broadcasted_iota(jnp.int32, (row_count, row_count), 1)
-    ).astype(jnp.bfloat16)
-    rank = jnp.dot(routed, before, preferred_element_type=jnp.float32)
-    slot = jnp.where(routed > 0, rank, -1.0).astype(jnp.int32)
-    return slot, row_weight
-
-
-UNIT_CHUNK = 256
-DOWN_CHUNKS = 4
-COPIES_AHEAD = 6
-
-
-def experts_kernel(
-    rows_ref, gain_ref, gate_hbm, up_hbm, down_hbm, out_ref,
-    gate_ref, up_ref, down_ref, normed_ref, act_ref, gate_sem, up_sem, down_sem,
-):
+    whole = pl.BlockSpec(memory_space=pltpu.VMEM)
+    return pl.pallas_call(
+        route_kernel,
+        out_shape=(
+            jax.ShapeDtypeStruct((experts_all, row_count), jnp.int32),
+            jax.ShapeDtypeStruct((experts_all, row_count), jnp.float32),
+            jax.ShapeDtypeStruct((row_count, chunk), residual_in.dtype),
+        ),
+        in_specs=[
+            pl.BlockSpec(memory_space=pltpu.SMEM), whole, whole, pl.BlockSpec(memory_space=pl.ANY),
+        ],
+        out_specs=(whole, whole, whole),
+        scratch_shapes=[pltpu.SemaphoreType.DMA],
+        compiler_params=pltpu.CompilerParams(vmem_limit_bytes=4 * 1024 * 1024),
+        name="route",
+    )(column, expert_ids.T, gate_scores.T, residual_in)
+
+
+def select_kernel(pieces_ref, residual_ref, slot_ref, hidden_ref, outgoing_ref):
+    sources = pieces_ref.shape[0]
+    experts, slots, chunk = outgoing_ref.shape
+    row_count = slot_ref.shape[1]
+    proj = pieces_ref[0].astype(jnp.float32)
+    for source in range(1, sources):
+        proj = proj + pieces_ref[source].astype(jnp.float32)
+    hidden = (residual_ref[...].astype(jnp.float32) + proj).astype(jnp.bfloat16)
+    hidden_ref[...] = hidden
+    group = row_count // slots
+    place = lax.broadcasted_iota(jnp.int32, (group, slots, row_count), 1)
+    for first in range(0, experts, group):
+        chosen = slot_ref[pl.ds(first, group), :][:, None, :] == place
+        selector = jnp.where(chosen, 1.0, 0.0).reshape(group * slots, row_count)
+        rows = jnp.dot(selector.astype(jnp.bfloat16), hidden, preferred_element_type=jnp.float32)
+        outgoing_ref[pl.ds(first, group)] = rows.astype(jnp.bfloat16).reshape(group, slots, chunk)
+
+
+def run_select(pieces, residual, slot, slots):
+    experts, row_count = slot.shape
+    chunk = pieces.shape[2]
+    whole = pl.BlockSpec(memory_space=pltpu.VMEM)
+    return pl.pallas_call(
+        select_kernel,
+        out_shape=(
+            jax.ShapeDtypeStruct((row_count, chunk), jnp.bfloat16),
+            jax.ShapeDtypeStruct((experts, slots, chunk), jnp.bfloat16),
+        ),
+        in_specs=[whole] * 3,
+        out_specs=(whole, whole),
+        compiler_params=pltpu.CompilerParams(vmem_limit_bytes=8 * 1024 * 1024),
+        cost_estimate=pl.CostEstimate(flops=100_000_000_000, bytes_accessed=4_000_000, transcendentals=0),
+        name="select",
+    )(pieces, residual, slot)
+
+
+def experts_kernel(rows_ref, gain_ref, gate_ref, up_ref, down_ref, out_ref, normed_ref, act_ref):
     replicas, pieces, slots, chunk = rows_ref.shape
     total = replicas * slots
     width = pieces * chunk
-    unit_chunks = gate_ref.shape[1] // UNIT_CHUNK
-    span = width // DOWN_CHUNKS
-
-    def unit_copies(i):
-        units = pl.ds(i * UNIT_CHUNK, UNIT_CHUNK)
-        return (
-            pltpu.make_async_copy(gate_hbm.at[:, units], gate_ref.at[:, units], gate_sem.at[i]),
-            pltpu.make_async_copy(up_hbm.at[:, units], up_ref.at[:, units], up_sem.at[i]),
-        )
-
-    def down_copy(i):
-        columns = pl.ds(i * span, span)
-        return pltpu.make_async_copy(
-            down_hbm.at[:, columns], down_ref.at[:, columns], down_sem.at[i]
-        )
-
-    order = [copy for i in range(unit_chunks) for copy in unit_copies(i)]
-    order += [down_copy(i) for i in range(DOWN_CHUNKS)]
-    for copy in order[:COPIES_AHEAD]:
-        copy.start()
-
-    def take(i):
-        order[i].wait()
-        if i + COPIES_AHEAD < len(order):
-            order[i + COPIES_AHEAD].start()
-
     squares = jnp.zeros((total, chunk), jnp.float32)
     for piece in range(pieces):
         part = rows_ref[:, piece].reshape(total, chunk).astype(jnp.float32)
@@ -227,49 +258,34 @@
         part = rows_ref[:, piece].reshape(total, chunk).astype(jnp.float32)
         columns = pl.ds(piece * chunk, chunk)
         normed_ref[:, columns] = (part * scale * gain_ref[:, columns]).astype(jnp.bfloat16)
-
-    for i in range(unit_chunks):
-        units = pl.ds(i * UNIT_CHUNK, UNIT_CHUNK)
-        take(2 * i)
-        gates = jnp.dot(normed_ref[...], gate_ref[:, units], preferred_element_type=jnp.float32)
-        take(2 * i + 1)
-        ups = jnp.dot(normed_ref[...], up_ref[:, units], preferred_element_type=jnp.float32)
-        act_ref[:, units] = (gates / (1.0 + jnp.exp(-gates)) * ups).astype(jnp.bfloat16)
-
-    per_copy = span // chunk
+    for first in range(0, gate_ref.shape[1], chunk):
+        units = pl.ds(first, chunk)
+        gate_part = jnp.dot(normed_ref[...], gate_ref[:, units], preferred_element_type=jnp.float32)
+        up_part = jnp.dot(normed_ref[...], up_ref[:, units], preferred_element_type=jnp.float32)
+        act_ref[:, units] = (gate_part / (1.0 + jnp.exp(-gate_part)) * up_part).astype(jnp.bfloat16)
     for piece in range(pieces):
-        if piece % per_copy == 0:
-            take(2 * unit_chunks + piece // per_copy)
         columns = pl.ds(piece * chunk, chunk)
         part = jnp.dot(act_ref[...], down_ref[:, columns], preferred_element_type=jnp.float32)
         out_ref[:, piece] = part.astype(jnp.bfloat16).reshape(replicas, slots, chunk)
 
 
-def run_experts(rows, norm_gain, w_gate, w_up, w_down):
+def run_experts(rows, norm_gain, weights):
     replicas, pieces, slots, chunk = rows.shape
-    width, hidden_units = w_gate.shape
+    width, hidden_units = weights[0].shape
     total = replicas * slots
-    unit_chunks = hidden_units // UNIT_CHUNK
     whole = pl.BlockSpec(memory_space=pltpu.VMEM)
-    left = pl.BlockSpec(memory_space=pltpu.HBM)
     return pl.pallas_call(
         experts_kernel,
         out_shape=jax.ShapeDtypeStruct(rows.shape, jnp.bfloat16),
-        in_specs=[whole, whole, left, left, left],
+        in_specs=[whole] * 5,
         out_specs=whole,
         scratch_shapes=[
-            pltpu.VMEM((width, hidden_units), jnp.bfloat16),
-            pltpu.VMEM((width, hidden_units), jnp.bfloat16),
-            pltpu.VMEM((hidden_units, width), jnp.bfloat16),
             pltpu.VMEM((total, width), jnp.bfloat16),
             pltpu.VMEM((total, hidden_units), jnp.bfloat16),
-            pltpu.SemaphoreType.DMA((unit_chunks,)),
-            pltpu.SemaphoreType.DMA((unit_chunks,)),
-            pltpu.SemaphoreType.DMA((DOWN_CHUNKS,)),
         ],
-        compiler_params=pltpu.CompilerParams(vmem_limit_bytes=60 * 1024 * 1024),
+        compiler_params=pltpu.CompilerParams(vmem_limit_bytes=16 * 1024 * 1024),
         name="experts",
-    )(rows, norm_gain.reshape(1, width), w_gate, w_up, w_down)
+    )(rows, norm_gain.reshape(1, width), *weights)
 
 
 def shards(
@@ -303,23 +319,21 @@
         out_weight, tensor_width,
     )
     pieces = lax.all_to_all(partial, "tensor", split_axis=0, concat_axis=0, tiled=True)
-    proj = jnp.sum(pieces.astype(jnp.float32), axis=0)
-    residual = lax.dynamic_slice_in_dim(residual_in, column * chunk, chunk, 1)
-    hidden = (residual.astype(jnp.float32) + proj).astype(jnp.bfloat16)
-
-    slot, row_weight = route(expert_ids, gate_scores, experts_all)
+    own_column = column.astype(jnp.int32).reshape(1)
+    slot, row_weight, residual = run_route(
+        own_column, expert_ids, gate_scores, residual_in, experts_all, chunk
+    )
+    hidden, outgoing = run_select(pieces, residual, slot, cap_slots)
+    received = lax.all_to_all(outgoing, both, split_axis=0, concat_axis=0, tiled=True)
+
+    weights = [w_gate[0], w_up[0], w_down[0]]
+    rows = received.reshape(replica_count, tensor_width, cap_slots, chunk)
+    answered = run_experts(rows, norm_gain, weights)
+    answered = answered.reshape(experts_all, cap_slots, chunk)
+    returned = lax.all_to_all(answered, both, split_axis=0, concat_axis=0, tiled=True)
+
     slot_axis = lax.broadcasted_iota(jnp.int32, (1, cap_slots, 1), 1)
     chosen = slot[:, None, :] == slot_axis
-    outgoing = jnp.einsum(
-        "esr,rj->esj", chosen.astype(jnp.bfloat16), hidden, preferred_element_type=jnp.float32
-    ).astype(jnp.bfloat16)
-    received = lax.all_to_all(outgoing, both, split_axis=0, concat_axis=0, tiled=True)
-
-    rows = received.reshape(replica_count, tensor_width, cap_slots, chunk)
-    answered = run_experts(rows, norm_gain, w_gate[0], w_up[0], w_down[0])
-    answered = answered.reshape(experts_all, cap_slots, chunk)
-    returned = lax.all_to_all(answered, both, split_axis=0, concat_axis=0, tiled=True)
-
     spread_weight = jnp.where(chosen, row_weight[:, None, :], 0.0)
     coarse = spread_weight.astype(jnp.bfloat16)
     fine = (spread_weight - coarse.astype(jnp.float32)).astype(jnp.bfloat16)

time: 108 us -> 102 us (0.944)
  Pallas kernels: 17.4 us -> 14.4 us
  other arithmetic: 1.63 us -> 0.01 us
    pallas_call x1, Pallas kernels: 9.62 us -> 3.85 us  [run_experts(): pl.pallas_call(experts_kernel, out_shape=jax.ShapeDtypeStruct(rows.shape,...]
    pallas_call x0 -> x2, Pallas kernels: none -> 2.18 us  [the longest x1 1.94 us: run_select(): pl.pallas_call(select_kernel, out_shape=(jax.ShapeDtypeStruct((row_count,...]
  transfers between devices with their start and end apart: 2 -> 2, of which waited for: 2 -> 2; matrix products, arithmetic and copies ran while one was open for 1% -> 0% of each run, Pallas kernels for 0% -> 0%
where the time goes in v4:
time: 102 us
  blocking collectives  37 us (36%)
  waiting for transfers between devices  36.3 us (36%)
  Pallas kernels  14.4 us (14%)
  starting transfers between devices  11.8 us (12%)
  matrix products  1.5 us (1%)
    all_to_all x1, blocking collectives, shards(): lax.all_to_all(outgoing, both, split_axis=0, concat_axis=0, tiled=True)  26.1 us
    all_to_all x1, waiting for transfers between devices, shards(): lax.all_to_all(answered, both, split_axis=0, concat_axis=0, tiled=True)  18.9 us
    all_to_all x1, waiting for transfers between devices, shards(): lax.all_to_all(partial, 'tensor', split_axis=0, concat_axis=0, tiled=True)  17.5 us
    all_to_all x1, blocking collectives, shards(): lax.all_to_all(layer.reshape(tensor_width, row_count // tensor_width, chu...  10.9 us
    pallas_call x1, Pallas kernels, run_attend(): pl.pallas_call(attend_kernel, out_shape=jax.ShapeDtypeStruct((pieces, row...  8.4 us
    all_to_all x1, starting transfers between devices, shards(): lax.all_to_all(partial, 'tensor', split_axis=0, concat_axis=0, tiled=True)  7.18 us
    all_to_all x1, starting transfers between devices, shards(): lax.all_to_all(answered, both, split_axis=0, concat_axis=0, tiled=True)  4.63 us
    pallas_call x1, Pallas kernels, run_experts(): pl.pallas_call(experts_kernel, out_shape=jax.ShapeDtypeStruct(rows.shape,...  3.85 us
  transfers between devices with their start and end apart: 2, of which 2 were waited for; matrix products, arithmetic and copies ran while one was open for 0% of the time, Pallas kernels for 0%

profile of v4, /device:TPU:0, one launch (start us, length us, event | category | flops | bytes accessed | tf_op | source)
XLA Modules:
  0.0 102.0 jit_solution(713538534545690024)
XLA Ops:
  0.0 0.0 copy-start.2
  0.0 8.4 %attend.1 = bf16[16,128,256]{2,1,0:T(8,128)(2,1)} custom-call(s32[1]{0:T(128)} %bitcast.head_ref, s32[128]{0:T(128)} %lengths_hbm.1, bf16[128,512]{1,0:T(8,128)(2,1)} %query_hbm.1, bf16[128,4,128]{2,1,0:T(4,128)(2,1)} %fresh_key_hbm.1, bf16[128,4,128]{2,1,0:T(4,128)(2,1)} %fresh_value_hbm.1, bf16[128,128,128]{2,1,0:T(8,128)(2,1)} %bitcast.38, ...), custom_call_target="tpu_custom_call" | custom-call | tf_op jit(solution)/shard_map/attend/pallas_call | solution.py:138
  8.4 7.2 %all-to-all-start = ((bf16[16,128,256]{2,1,0:T(8,128)(2,1)}), bf16[16,128,256]{2,1,0:T(8,128)(2,1)}, u32[]{:S(2)}, u32[]{:S(2)}) async-start(bf16[16,128,256]{2,1,0:T(8,128)(2,1)} %attend.1), calls=%async_computation | async-start | bytes 2097152 | tf_op jit(solution)/shard_map/all_to_all | solution.py:321
  15.6 0.0 copy-done.2
  15.6 0.0 copy-done.4
  15.6 0.0 copy-done.5
  15.6 0.2 route.1
  15.9 17.5 %all-to-all-done.pieces_ref = bf16[16,128,256]{2,1,0:T(8,128)(2,1)} async-done(((bf16[16,128,256]{2,1,0:T(8,128)(2,1)}), bf16[16,128,256]{2,1,0:T(8,128)(2,1)}, u32[]{:S(2)}, u32[]{:S(2)}) %all-to-all-start) | async-done | bytes 1048608 | tf_op jit(solution)/shard_map/all_to_all | solution.py:321
  33.4 1.9 %select.5 = (bf16[128,256]{1,0:T(8,128)(2,1)S(1)}, bf16[128,16,256]{2,1,0:T(8,128)(2,1)S(1)}) custom-call(bf16[16,128,256]{2,1,0:T(8,128)(2,1)} %all-to-all-done.pieces_ref, bf16[128,256]{1,0:T(8,128)(2,1)S(1)} %get-tuple-element.10.residual_ref, s32[128,128]{1,0:T(8,128)S(1)} %get-tuple-element.11.slot_ref), custom_call_target="tpu_custom_call" | custom-call | flops 99999997952 | bytes 4000000 | tf_op jit(solution)/shard_map/select/pallas_call | solution.py:233
  35.3 26.1 %all_to_all.20 = bf16[128,16,256]{2,1,0:T(8,128)(2,1)S(1)} all-to-all(bf16[128,16,256]{2,1,0:T(8,128)(2,1)S(1)} %get-tuple-element.14), channel_id=1, replica_groups=mesh['dp'=8,'tensor'=16] {'dp','tensor'}, dimensions={0} | all-to-all | bytes 2097152 | tf_op jit(solution)/shard_map/all_to_all | solution.py:327
  61.5 0.0 slice-done
  61.5 0.0 slice-done.1
  61.5 0.0 copy-done
  61.5 0.0 copy-done.1
  61.5 0.0 copy-done.3
  61.5 3.9 %experts.1 = bf16[8,16,16,256]{3,2,1,0:T(8,128)(2,1)} custom-call(bf16[8,16,16,256]{3,2,1,0:T(8,128)(2,1)S(1)} %bitcast.34, f32[1,4096]{1,0:T(1,128)S(1)} %bitcast.35, bf16[4096,768]{1,0:T(8,128)(2,1)S(1)} %bitcast.31, bf16[4096,768]{1,0:T(8,128)(2,1)S(1)} %bitcast.32, bf16[768,4096]{1,0:T(8,128)(2,1)S(1)} %bitcast.33), custom_call_target="tpu_custom_call" | custom-call | tf_op jit(solution)/shard_map/experts/pallas_call | solution.py:277
  65.4 4.6 %all-to-all-start.2 = ((bf16[128,16,256]{2,1,0:T(8,128)(2,1)}), bf16[128,16,256]{2,1,0:T(8,128)(2,1)S(1)}, u32[]{:S(2)}, u32[]{:S(2)}) async-start(bf16[128,16,256]{2,1,0:T(8,128)(2,1)} %bitcast.11), calls=%async_computation.2 | async-start | bytes 2097152 | tf_op jit(solution)/shard_map/all_to_all | solution.py:333
  70.0 0.1 copy.18
  70.1 0.1 copy.19
  70.2 18.9 %all-to-all-done.2 = bf16[128,16,256]{2,1,0:T(8,128)(2,1)S(1)} async-done(((bf16[128,16,256]{2,1,0:T(8,128)(2,1)}), bf16[128,16,256]{2,1,0:T(8,128)(2,1)S(1)}, u32[]{:S(2)}, u32[]{:S(2)}) %all-to-all-start.2) | async-done | bytes 1048608 | tf_op jit(solution)/shard_map/all_to_all | solution.py:333
  89.0 0.8 convolution_bitcast_fusion
  89.8 0.7 fusion.3
  90.6 10.9 %all_to_all.21 = bf16[16,8,256]{2,1,0:T(8,128)(2,1)S(1)} all-to-all(bf16[16,8,256]{2,1,0:T(8,128)(2,1)S(1)} %fusion.3), channel_id=1, replica_groups=mesh['dp'=8,'tensor'=16] {'tensor'}, dimensions={0} | all-to-all | bytes 131072 | tf_op jit(solution)/shard_map/all_to_all | solution.py:344
  101.4 0.6 copy.27
  (8 shorter events, 0.0 us)
Async XLA Ops:
  0.0 15.6 %copy-start.2 = (bf16[128,4096]{1,0:T(8,128)(2,1)S(1)}, bf16[128,4096]{1,0:T(8,128)(2,1)}, u32[]{:S(2)}) copy-start(bf16[128,4096]{1,0:T(8,128)(2,1)} %residual_hbm.1) | copy-start | bytes 3145732
  0.0 15.6 %copy-start.4 = (s32[128,8]{0,1:T(8,128)S(1)}, s32[128,8]{0,1:T(8,128)}, u32[]{:S(2)}) copy-start(s32[128,8]{0,1:T(8,128)} %param.23) | copy-start | bytes 12292
  0.0 15.6 %copy-start.5 = (f32[128,8]{0,1:T(8,128)S(1)}, f32[128,8]{0,1:T(8,128)}, u32[]{:S(2)}) copy-start(f32[128,8]{0,1:T(8,128)} %param.24) | copy-start | bytes 12292
  0.0 61.5 %slice-start = ((s8[6291456]{0:T(1024)(128)(4,1)}), s8[2097152]{0:T(1024)(128)(4,1)S(1)}, s32[]{:S(2)}) async-start(s8[6291456]{0:T(1024)(128)(4,1)} %bitcast.29), calls=%async_computation.4 | async-start | bytes 4194304
  8.4 24.9 %all-to-all-start = ((bf16[16,128,256]{2,1,0:T(8,128)(2,1)}), bf16[16,128,256]{2,1,0:T(8,128)(2,1)}, u32[]{:S(2)}, u32[]{:S(2)}) async-start(bf16[16,128,256]{2,1,0:T(8,128)(2,1)} %attend.1), calls=%async_computation | async-start | bytes 2097152 | tf_op jit(solution)/shard_map/all_to_all | solution.py:321
  33.4 28.1 %slice-start.1 = ((s8[6291456]{0:T(1024)(128)(4,1)}), s8[4194304]{0:T(1024)(128)(4,1)S(1)}, s32[]{:S(2)}) async-start(s8[6291456]{0:T(1024)(128)(4,1)} %bitcast.29), calls=%async_computation.5 | async-start | bytes 8388608
  33.4 28.1 %copy-start = (bf16[1,4096,768]{2,1,0:T(8,128)(2,1)S(1)}, bf16[1,4096,768]{2,1,0:T(8,128)(2,1)}, u32[]{:S(2)}) copy-start(bf16[1,4096,768]{2,1,0:T(8,128)(2,1)} %param.26) | copy-start | bytes 18874372
  33.4 28.1 %copy-start.1 = (bf16[1,768,4096]{2,1,0:T(8,128)(2,1)S(1)}, bf16[1,768,4096]{2,1,0:T(8,128)(2,1)}, u32[]{:S(2)}) copy-start(bf16[1,768,4096]{2,1,0:T(8,128)(2,1)} %param.27) | copy-start | bytes 18874372
  33.4 28.1 %copy-start.3 = (f32[4096]{0:T(1024)S(1)}, f32[4096]{0:T(1024)}, u32[]{:S(2)}) copy-start(f32[4096]{0:T(1024)} %param.22) | copy-start | bytes 49156
  65.4 23.7 %all-to-all-start.2 = ((bf16[128,16,256]{2,1,0:T(8,128)(2,1)}), bf16[128,16,256]{2,1,0:T(8,128)(2,1)S(1)}, u32[]{:S(2)}, u32[]{:S(2)}) async-start(bf16[128,16,256]{2,1,0:T(8,128)(2,1)} %bitcast.11), calls=%async_computation.2 | async-start | bytes 2097152 | tf_op jit(solution)/shard_map/all_to_all | solution.py:333

commit v5 on v4

--- a/solution.py
+++ b/solution.py
@@ -8,21 +8,19 @@
 
 ROWS_STEP = 32
 STEPS_AHEAD = 3
-WEIGHT_COPIES = 4
 
 
 def attend_kernel(
-    head_ref, lengths_hbm, query_hbm, fresh_key_hbm, fresh_value_hbm, key_hbm, value_hbm, weight_hbm,
-    out_ref,
+    head_ref, column_ref, lengths_hbm, residual_hbm, query_hbm, fresh_key_hbm, fresh_value_hbm, key_hbm, value_hbm, weight_hbm,
+    out_ref, residual_ref,
     lengths_ref, query_ref, fresh_key_ref, fresh_value_ref, key_ref, value_ref, weight_ref,
     query_scr, own_key_scr, own_value_scr, attended_scr, heads_scr,
-    small_sem, key_sem, value_sem, weight_sem,
+    small_sem, residual_sem, key_sem, value_sem, weight_sem,
 ):
     row_count, positions, head_size = key_ref.shape
     head_count = query_ref.shape[1] // head_size
     pieces, _, chunk = out_ref.shape
     steps = row_count // ROWS_STEP
-    width = weight_ref.shape[0] // WEIGHT_COPIES
     score_scale = head_size ** (-0.5)
 
     def cache_copies(step):
@@ -32,10 +30,9 @@
             pltpu.make_async_copy(value_hbm.at[rows], value_ref.at[rows], value_sem.at[step]),
         )
 
-    def weight_copy(i):
-        rows = pl.ds(i * width, width)
-        return pltpu.make_async_copy(weight_hbm.at[rows], weight_ref.at[rows], weight_sem.at[i])
-
+    weight_copy = pltpu.make_async_copy(weight_hbm, weight_ref, weight_sem)
+    own = pl.ds(pl.multiple_of(column_ref[0] * chunk, chunk), chunk)
+    residual_copy = pltpu.make_async_copy(residual_hbm.at[:, own], residual_ref, residual_sem)
     small = [
         pltpu.make_async_copy(query_hbm, query_ref, small_sem.at[0]),
         pltpu.make_async_copy(fresh_key_hbm, fresh_key_ref, small_sem.at[1]),
@@ -74,9 +71,10 @@
             for copy in cache_copies(step + STEPS_AHEAD):
                 copy.start()
 
-        @pl.when(step + WEIGHT_COPIES >= steps)
+        @pl.when(step == 0)
         def _():
-            weight_copy(step + WEIGHT_COPIES - steps).start()
+            weight_copy.start()
+            residual_copy.start()
 
         first = pl.multiple_of(step * (ROWS_STEP * head_count), ROWS_STEP * head_count)
         queries = query_scr[pl.ds(first, ROWS_STEP * head_count), :]
@@ -117,8 +115,8 @@
         columns = pl.ds(head * head_size, head_size)
         rows = pl.ds(head, row_count, stride=head_count)
         heads_scr[:, columns] = attended_scr[rows, :].astype(jnp.bfloat16)
-    for i in range(WEIGHT_COPIES):
-        weight_copy(i).wait()
+    residual_copy.wait()
+    weight_copy.wait()
     for piece in range(pieces):
         columns = pl.ds(piece * chunk, chunk)
         part = jnp.dot(
@@ -127,7 +125,9 @@
         out_ref[piece] = part.astype(jnp.bfloat16)
 
 
-def run_attend(query, fresh_key, fresh_value, key_cache, value_cache, lengths, kv_head, out_weight, pieces):
+def run_attend(
+    residual_in, query, fresh_key, fresh_value, key_cache, value_cache, lengths, column, kv_head, out_weight, pieces,
+):
     row_count, positions, head_size = key_cache.shape
     width = out_weight.shape[1]
     many = query.shape[0] * query.shape[1] // head_size
@@ -137,9 +137,12 @@
     steps = row_count // ROWS_STEP
     return pl.pallas_call(
         attend_kernel,
-        out_shape=jax.ShapeDtypeStruct((pieces, row_count, width // pieces), jnp.bfloat16),
-        in_specs=[scalars] + [left] * 7,
-        out_specs=whole,
+        out_shape=(
+            jax.ShapeDtypeStruct((pieces, row_count, width // pieces), jnp.bfloat16),
+            jax.ShapeDtypeStruct((row_count, width // pieces), residual_in.dtype),
+        ),
+        in_specs=[scalars] * 2 + [left] * 8,
+        out_specs=(whole, whole),
         scratch_shapes=[
             pltpu.SMEM(lengths.shape, jnp.int32),
             pltpu.VMEM(query.shape, jnp.bfloat16),
@@ -154,21 +157,18 @@
             pltpu.VMEM((many, head_size), jnp.float32),
             pltpu.VMEM(query.shape, jnp.bfloat16),
             pltpu.SemaphoreType.DMA((4,)),
+            pltpu.SemaphoreType.DMA,
             pltpu.SemaphoreType.DMA((steps,)),
             pltpu.SemaphoreType.DMA((steps,)),
-            pltpu.SemaphoreType.DMA((WEIGHT_COPIES,)),
+            pltpu.SemaphoreType.DMA,
         ],
         compiler_params=pltpu.CompilerParams(vmem_limit_bytes=60 * 1024 * 1024),
         name="attend",
-    )(kv_head, lengths, query, fresh_key, fresh_value, key_cache, value_cache, out_weight)
-
-
-def route_kernel(column_ref, ids_ref, scores_ref, residual_hbm, slot_ref, weight_ref, residual_ref, sem):
+    )(kv_head, column, lengths, residual_in, query, fresh_key, fresh_value, key_cache, value_cache, out_weight)
+
+
+def route_kernel(ids_ref, scores_ref, residual_ref, slot_ref, weight_ref, kept_ref):
     experts, row_count = slot_ref.shape
-    chunk = residual_ref.shape[1]
-    own = pl.ds(pl.multiple_of(column_ref[0] * chunk, chunk), chunk)
-    copy = pltpu.make_async_copy(residual_hbm.at[:, own], residual_ref, sem)
-    copy.start()
     topk = ids_ref.shape[0]
     scores = scores_ref[...]
     weights = scores / jnp.sum(scores, axis=0, keepdims=True)
@@ -185,10 +185,10 @@
     rank = jnp.dot(named.astype(jnp.bfloat16), before, preferred_element_type=jnp.float32)
     slot_ref[...] = jnp.where(named > 0.0, rank, -1.0).astype(jnp.int32)
     weight_ref[...] = weight
-    copy.wait()
-
-
-def run_route(column, expert_ids, gate_scores, residual_in, experts_all, chunk):
+    kept_ref[...] = residual_ref[...]
+
+
+def run_route(expert_ids, gate_scores, residual, experts_all):
     row_count = expert_ids.shape[0]
     whole = pl.BlockSpec(memory_space=pltpu.VMEM)
     return pl.pallas_call(
@@ -196,16 +196,13 @@
         out_shape=(
             jax.ShapeDtypeStruct((experts_all, row_count), jnp.int32),
             jax.ShapeDtypeStruct((experts_all, row_count), jnp.float32),
-            jax.ShapeDtypeStruct((row_count, chunk), residual_in.dtype),
+            jax.ShapeDtypeStruct(residual.shape, residual.dtype),
         ),
-        in_specs=[
-            pl.BlockSpec(memory_space=pltpu.SMEM), whole, whole, pl.BlockSpec(memory_space=pl.ANY),
-        ],
+        in_specs=[whole] * 3,
         out_specs=(whole, whole, whole),
-        scratch_shapes=[pltpu.SemaphoreType.DMA],
         compiler_params=pltpu.CompilerParams(vmem_limit_bytes=4 * 1024 * 1024),
         name="route",
-    )(column, expert_ids.T, gate_scores.T, residual_in)
+    )(expert_ids.T, gate_scores.T, residual)
 
 
 def select_kernel(pieces_ref, residual_ref, slot_ref, hidden_ref, outgoing_ref):
@@ -239,7 +236,7 @@
         in_specs=[whole] * 3,
         out_specs=(whole, whole),
         compiler_params=pltpu.CompilerParams(vmem_limit_bytes=8 * 1024 * 1024),
-        cost_estimate=pl.CostEstimate(flops=100_000_000_000, bytes_accessed=4_000_000, transcendentals=0),
+        cost_estimate=pl.CostEstimate(flops=115_000_000_000, bytes_accessed=4_000_000, transcendentals=0),
         name="select",
     )(pieces, residual, slot)
 
@@ -314,15 +311,13 @@
     cap_slots = 2 * max(1, row_count * expert_ids.shape[1] // experts_all)
 
     kv_head = (column // (tensor_width // fresh_key.shape[1])).astype(jnp.int32).reshape(1)
-    partial = run_attend(
-        query, fresh_key, fresh_value, key_cache[:, 0], value_cache[:, 0], lengths, kv_head,
-        out_weight, tensor_width,
+    own_column = column.astype(jnp.int32).reshape(1)
+    partial, residual = run_attend(
+        residual_in, query, fresh_key, fresh_value, key_cache[:, 0], value_cache[:, 0], lengths,
+        own_column, kv_head, out_weight, tensor_width,
     )
     pieces = lax.all_to_all(partial, "tensor", split_axis=0, concat_axis=0, tiled=True)
-    own_column = column.astype(jnp.int32).reshape(1)
-    slot, row_weight, residual = run_route(
-        own_column, expert_ids, gate_scores, residual_in, experts_all, chunk
-    )
+    slot, row_weight, residual = run_route(expert_ids, gate_scores, residual, experts_all)
     hidden, outgoing = run_select(pieces, residual, slot, cap_slots)
     received = lax.all_to_all(outgoing, both, split_axis=0, concat_axis=0, tiled=True)
 

time: 102 us -> 100 us (0.980)
  Pallas kernels: 14.4 us -> 12.1 us
    pallas_call x1, Pallas kernels: 1.94 us -> 0.56 us  [run_select(): pl.pallas_call(select_kernel, out_shape=(jax.ShapeDtypeStruct((row_count,...]
where the time goes in v5:
time: 100 us; the launch traced here: 99.6 us
  blocking collectives  37 us (37%)
  waiting for transfers between devices  35.5 us (36%)
  Pallas kernels  12.1 us (12%)
  starting transfers between devices  11.8 us (12%)
  local copies, waits for them, and re-layouts  1.67 us (2%)
  matrix products  1.5 us (2%)
    all_to_all x1, blocking collectives, shards(): lax.all_to_all(outgoing, both, split_axis=0, concat_axis=0, tiled=True)  26.2 us
    all_to_all x1, waiting for transfers between devices, shards(): lax.all_to_all(answered, both, split_axis=0, concat_axis=0, tiled=True)  18.9 us
    all_to_all x1, waiting for transfers between devices, shards(): lax.all_to_all(partial, 'tensor', split_axis=0, concat_axis=0, tiled=True)  16.6 us
    all_to_all x1, blocking collectives, shards(): lax.all_to_all(layer.reshape(tensor_width, row_count // tensor_width, chu...  10.9 us
    pallas_call x1, Pallas kernels, run_attend(): pl.pallas_call(attend_kernel, out_shape=(jax.ShapeDtypeStruct((pieces, ro...  7.47 us
    all_to_all x1, starting transfers between devices, shards(): lax.all_to_all(partial, 'tensor', split_axis=0, concat_axis=0, tiled=True)  7.14 us
    all_to_all x1, starting transfers between devices, shards(): lax.all_to_all(answered, both, split_axis=0, concat_axis=0, tiled=True)  4.63 us
    pallas_call x1, Pallas kernels, run_experts(): pl.pallas_call(experts_kernel, out_shape=jax.ShapeDtypeStruct(rows.shape,...  3.84 us
  transfers between devices with their start and end apart: 2, of which 2 were waited for; matrix products, arithmetic and copies ran while one was open for 0% of the time, Pallas kernels for 0%

profile of v5, /device:TPU:0, one launch (start us, length us, event | category | flops | bytes accessed | tf_op | source)
XLA Modules:
  0.0 99.6 jit_solution(470204999574142091)
XLA Ops:
  0.0 7.5 %attend.1 = (bf16[16,128,256]{2,1,0:T(8,128)(2,1)}, bf16[128,256]{1,0:T(8,128)(2,1)}) custom-call(s32[1]{0:T(128)} %bitcast.head_ref, s32[1]{0:T(128)} %bitcast.1.column_ref, s32[128]{0:T(128)} %lengths_hbm.1, bf16[128,4096]{1,0:T(8,128)(2,1)} %residual_hbm.1, bf16[128,512]{1,0:T(8,128)(2,1)} %query_hbm.1, bf16[128,4,128]{2,1,0:T(4,128)(2,1)} %fresh_key_hbm.1, ...), custom_call_target="tpu_custom_call" | custom-call | tf_op jit(solution)/shard_map/attend/pallas_call | solution.py:138
  7.5 7.1 %all-to-all-start = ((bf16[16,128,256]{2,1,0:T(8,128)(2,1)}), bf16[16,128,256]{2,1,0:T(8,128)(2,1)S(1)}, u32[]{:S(2)}, u32[]{:S(2)}) async-start(bf16[16,128,256]{2,1,0:T(8,128)(2,1)} %get-tuple-element.12), calls=%async_computation | async-start | bytes 2097152 | tf_op jit(solution)/shard_map/all_to_all | solution.py:319
  14.6 0.0 copy-done.4
  14.6 0.0 copy-done.5
  14.7 0.0 copy-start.2
  14.7 0.8 copy-done.2
  15.5 0.2 route.1
  15.7 16.6 %all-to-all-done.pieces_ref = bf16[16,128,256]{2,1,0:T(8,128)(2,1)S(1)} async-done(((bf16[16,128,256]{2,1,0:T(8,128)(2,1)}), bf16[16,128,256]{2,1,0:T(8,128)(2,1)S(1)}, u32[]{:S(2)}, u32[]{:S(2)}) %all-to-all-start) | async-done | bytes 1048608 | tf_op jit(solution)/shard_map/all_to_all | solution.py:319
  32.3 0.6 select.5
  32.9 26.2 %all_to_all.20 = bf16[128,16,256]{2,1,0:T(8,128)(2,1)S(1)} all-to-all(bf16[128,16,256]{2,1,0:T(8,128)(2,1)S(1)} %get-tuple-element.18), channel_id=1, replica_groups=mesh['dp'=8,'tensor'=16] {'dp','tensor'}, dimensions={0} | all-to-all | bytes 2097152 | tf_op jit(solution)/shard_map/all_to_all | solution.py:322
  59.1 0.0 slice-done
  59.1 0.0 slice-done.1
  59.1 0.0 copy-done
  59.1 0.0 copy-done.1
  59.1 0.0 copy-done.3
  59.1 3.8 %experts.1 = bf16[8,16,16,256]{3,2,1,0:T(8,128)(2,1)} custom-call(bf16[8,16,16,256]{3,2,1,0:T(8,128)(2,1)S(1)} %bitcast.34, f32[1,4096]{1,0:T(1,128)S(1)} %bitcast.35, bf16[4096,768]{1,0:T(8,128)(2,1)S(1)} %bitcast.31, bf16[4096,768]{1,0:T(8,128)(2,1)S(1)} %bitcast.32, bf16[768,4096]{1,0:T(8,128)(2,1)S(1)} %bitcast.33), custom_call_target="tpu_custom_call" | custom-call | tf_op jit(solution)/shard_map/experts/pallas_call | solution.py:274
  62.9 4.6 %all-to-all-start.2 = ((bf16[128,16,256]{2,1,0:T(8,128)(2,1)}), bf16[128,16,256]{2,1,0:T(8,128)(2,1)S(1)}, u32[]{:S(2)}, u32[]{:S(2)}) async-start(bf16[128,16,256]{2,1,0:T(8,128)(2,1)} %bitcast.11), calls=%async_computation.2 | async-start | bytes 2097152 | tf_op jit(solution)/shard_map/all_to_all | solution.py:328
  67.6 0.1 copy.18
  67.7 0.1 copy.19
  67.8 18.9 %all-to-all-done.2 = bf16[128,16,256]{2,1,0:T(8,128)(2,1)S(1)} async-done(((bf16[128,16,256]{2,1,0:T(8,128)(2,1)}), bf16[128,16,256]{2,1,0:T(8,128)(2,1)S(1)}, u32[]{:S(2)}, u32[]{:S(2)}) %all-to-all-start.2) | async-done | bytes 1048608 | tf_op jit(solution)/shard_map/all_to_all | solution.py:328
  86.6 0.8 convolution_bitcast_fusion
  87.4 0.7 fusion.3
  88.1 10.9 %all_to_all.21 = bf16[16,8,256]{2,1,0:T(8,128)(2,1)S(1)} all-to-all(bf16[16,8,256]{2,1,0:T(8,128)(2,1)S(1)} %fusion.3), channel_id=1, replica_groups=mesh['dp'=8,'tensor'=16] {'tensor'}, dimensions={0} | all-to-all | bytes 131072 | tf_op jit(solution)/shard_map/all_to_all | solution.py:339
  99.0 0.6 copy.27
  (8 shorter events, 0.0 us)
Async XLA Ops:
  0.0 14.6 %copy-start.4 = (s32[128,8]{0,1:T(8,128)S(1)}, s32[128,8]{0,1:T(8,128)}, u32[]{:S(2)}) copy-start(s32[128,8]{0,1:T(8,128)} %param.23) | copy-start | bytes 12292
  0.0 14.6 %copy-start.5 = (f32[128,8]{0,1:T(8,128)S(1)}, f32[128,8]{0,1:T(8,128)}, u32[]{:S(2)}) copy-start(f32[128,8]{0,1:T(8,128)} %param.24) | copy-start | bytes 12292
  0.0 59.1 %slice-start = ((s8[6291456]{0:T(1024)(128)(4,1)}), s8[2097152]{0:T(1024)(128)(4,1)S(1)}, s32[]{:S(2)}) async-start(s8[6291456]{0:T(1024)(128)(4,1)} %bitcast.29), calls=%async_computation.4 | async-start | bytes 4194304
  7.5 24.8 %all-to-all-start = ((bf16[16,128,256]{2,1,0:T(8,128)(2,1)}), bf16[16,128,256]{2,1,0:T(8,128)(2,1)S(1)}, u32[]{:S(2)}, u32[]{:S(2)}) async-start(bf16[16,128,256]{2,1,0:T(8,128)(2,1)} %get-tuple-element.12), calls=%async_computation | async-start | bytes 2097152 | tf_op jit(solution)/shard_map/all_to_all | solution.py:319
  14.7 0.8 copy-start.2
  32.3 26.7 %slice-start.1 = ((s8[6291456]{0:T(1024)(128)(4,1)}), s8[4194304]{0:T(1024)(128)(4,1)S(1)}, s32[]{:S(2)}) async-start(s8[6291456]{0:T(1024)(128)(4,1)} %bitcast.29), calls=%async_computation.5 | async-start | bytes 8388608
  32.3 26.7 %copy-start = (bf16[1,4096,768]{2,1,0:T(8,128)(2,1)S(1)}, bf16[1,4096,768]{2,1,0:T(8,128)(2,1)}, u32[]{:S(2)}) copy-start(bf16[1,4096,768]{2,1,0:T(8,128)(2,1)} %param.26) | copy-start | bytes 18874372
  32.3 26.7 %copy-start.1 = (bf16[1,768,4096]{2,1,0:T(8,128)(2,1)S(1)}, bf16[1,768,4096]{2,1,0:T(8,128)(2,1)}, u32[]{:S(2)}) copy-start(bf16[1,768,4096]{2,1,0:T(8,128)(2,1)} %param.27) | copy-start | bytes 18874372
  32.3 26.8 %copy-start.3 = (f32[4096]{0:T(1024)S(1)}, f32[4096]{0:T(1024)}, u32[]{:S(2)}) copy-start(f32[4096]{0:T(1024)} %param.22) | copy-start | bytes 49156
  62.9 23.7 %all-to-all-start.2 = ((bf16[128,16,256]{2,1,0:T(8,128)(2,1)}), bf16[128,16,256]{2,1,0:T(8,128)(2,1)S(1)}, u32[]{:S(2)}, u32[]{:S(2)}) async-start(bf16[128,16,256]{2,1,0:T(8,128)(2,1)} %bitcast.11), calls=%async_computation.2 | async-start | bytes 2097152 | tf_op jit(solution)/shard_map/all_to_all | solution.py:328

commit v6 on v5

--- a/solution.py
+++ b/solution.py
@@ -201,6 +201,9 @@
         in_specs=[whole] * 3,
         out_specs=(whole, whole, whole),
         compiler_params=pltpu.CompilerParams(vmem_limit_bytes=4 * 1024 * 1024),
+        cost_estimate=pl.CostEstimate(
+            flops=60_000_000_000, bytes_accessed=4_000_000, transcendentals=0
+        ),
         name="route",
     )(expert_ids.T, gate_scores.T, residual)
 
@@ -283,6 +286,66 @@
         compiler_params=pltpu.CompilerParams(vmem_limit_bytes=16 * 1024 * 1024),
         name="experts",
     )(rows, norm_gain.reshape(1, width), *weights)
+
+
+def spread_kernel(slot_ref, weight_ref, spread_ref):
+    experts, row_count = slot_ref.shape
+    total = spread_ref.shape[2]
+    slots = total // experts
+    step = 256
+    slot = slot_ref[...].astype(jnp.float32).T.astype(jnp.bfloat16)
+    weight = weight_ref[...].T
+    coarse = weight.astype(jnp.bfloat16)
+    fine = (weight - coarse.astype(jnp.float32)).astype(jnp.bfloat16)
+    begin = lax.broadcasted_iota(jnp.int32, (experts, step), 0) * slots
+    place = lax.broadcasted_iota(jnp.int32, (experts, step), 1)
+    lane = lax.broadcasted_iota(jnp.int32, (row_count, step), 1)
+    for first in range(0, total, step):
+        inside = (place + first >= begin) & (place + first < begin + slots)
+        expand = jnp.where(inside, 1.0, 0.0).astype(jnp.bfloat16)
+        here = jnp.dot(slot, expand, preferred_element_type=jnp.float32)
+        chosen = here == lax.rem(lane + first, slots).astype(jnp.float32)
+        for part, values in enumerate((coarse, fine)):
+            spread = jnp.dot(values, expand, preferred_element_type=jnp.float32)
+            spread_ref[part, :, pl.ds(first, step)] = jnp.where(chosen, spread, 0.0).astype(
+                jnp.bfloat16
+            )
+
+
+def run_spread(slot, row_weight, slots):
+    experts, row_count = slot.shape
+    whole = pl.BlockSpec(memory_space=pltpu.VMEM)
+    return pl.pallas_call(
+        spread_kernel,
+        out_shape=jax.ShapeDtypeStruct((2, row_count, experts * slots), jnp.bfloat16),
+        in_specs=[whole] * 2,
+        out_specs=whole,
+        compiler_params=pltpu.CompilerParams(vmem_limit_bytes=4 * 1024 * 1024),
+        name="spread",
+    )(slot, row_weight)
+
+
+def combine_kernel(spread_ref, returned_ref, hidden_ref, out_ref):
+    experts, slots, chunk = returned_ref.shape
+    rows = returned_ref[...].reshape(experts * slots, chunk)
+    mixture = jnp.dot(spread_ref[0], rows, preferred_element_type=jnp.float32) + jnp.dot(
+        spread_ref[1], rows, preferred_element_type=jnp.float32
+    )
+    layer = hidden_ref[...].astype(jnp.float32) + mixture
+    out_ref[...] = layer.reshape(out_ref.shape).astype(jnp.bfloat16)
+
+
+def run_combine(spread, returned, hidden, parts):
+    row_count, chunk = hidden.shape
+    whole = pl.BlockSpec(memory_space=pltpu.VMEM)
+    return pl.pallas_call(
+        combine_kernel,
+        out_shape=jax.ShapeDtypeStruct((parts, row_count // parts, chunk), jnp.bfloat16),
+        in_specs=[whole] * 3,
+        out_specs=whole,
+        compiler_params=pltpu.CompilerParams(vmem_limit_bytes=4 * 1024 * 1024),
+        name="combine",
+    )(spread, returned, hidden)
 
 
 def shards(
@@ -325,19 +388,11 @@
     rows = received.reshape(replica_count, tensor_width, cap_slots, chunk)
     answered = run_experts(rows, norm_gain, weights)
     answered = answered.reshape(experts_all, cap_slots, chunk)
+    slot, row_weight, answered = lax.optimization_barrier((slot, row_weight, answered))
     returned = lax.all_to_all(answered, both, split_axis=0, concat_axis=0, tiled=True)
-
-    slot_axis = lax.broadcasted_iota(jnp.int32, (1, cap_slots, 1), 1)
-    chosen = slot[:, None, :] == slot_axis
-    spread_weight = jnp.where(chosen, row_weight[:, None, :], 0.0)
-    coarse = spread_weight.astype(jnp.bfloat16)
-    fine = (spread_weight - coarse.astype(jnp.float32)).astype(jnp.bfloat16)
-    mixture = jnp.einsum(
-        "esr,esj->rj", coarse, returned, preferred_element_type=jnp.float32
-    ) + jnp.einsum("esr,esj->rj", fine, returned, preferred_element_type=jnp.float32)
-    layer = (hidden.astype(jnp.float32) + mixture).astype(jnp.bfloat16)
+    spread = run_spread(slot, row_weight, cap_slots)
     own = lax.all_to_all(
-        layer.reshape(tensor_width, row_count // tensor_width, chunk),
+        run_combine(spread, returned, hidden, tensor_width),
         "tensor",
         split_axis=0,
         concat_axis=0,

time: 100 us -> 98.3 us (0.983)
  matrix products: 1.5 us -> 0 us
    dot_general x2 -> x0, matrix products: 1.5 us -> none  [the longest x1 0.76 us: shards(): jnp.einsum('esr,esj->rj', fine, returned, preferred_element_type=jnp.floa...]
    pallas_call x0 -> x2, Pallas kernels: none -> 1.12 us  [the longest x1 0.67 us: run_spread(): pl.pallas_call(spread_kernel, out_shape=jax.ShapeDtypeStruct((2, row_coun...]
  transfers between devices with their start and end apart: 2 -> 2, of which waited for: 2 -> 2; matrix products, arithmetic and copies ran while one was open for 0% -> 0% of each run, Pallas kernels for 0% -> 1%
where the time goes in v6:
time: 98.3 us; the launch traced here: 98 us
  blocking collectives  37 us (38%)
  waiting for transfers between devices  35 us (36%)
  Pallas kernels  12.7 us (13%)
  starting transfers between devices  11.8 us (12%)
  local copies, waits for them, and re-layouts  1.49 us (2%)
    all_to_all x1, blocking collectives, shards(): lax.all_to_all(outgoing, both, split_axis=0, concat_axis=0, tiled=True)  26.1 us
    all_to_all x1, waiting for transfers between devices, shards(): lax.all_to_all(answered, both, split_axis=0, concat_axis=0, tiled=True)  18.4 us
    all_to_all x1, waiting for transfers between devices, shards(): lax.all_to_all(partial, 'tensor', split_axis=0, concat_axis=0, tiled=True)  16.6 us
    all_to_all x1, blocking collectives, shards(): lax.all_to_all(run_combine(spread, returned, hidden, tensor_width), 'tens...  10.9 us
    all_to_all x1, starting transfers between devices, shards(): lax.all_to_all(partial, 'tensor', split_axis=0, concat_axis=0, tiled=True)  7.13 us
    pallas_call x1, Pallas kernels, run_attend(): pl.pallas_call(attend_kernel, out_shape=(jax.ShapeDtypeStruct((pieces, ro...  6.9 us
    all_to_all x1, starting transfers between devices, shards(): lax.all_to_all(answered, both, split_axis=0, concat_axis=0, tiled=True)  4.63 us
    pallas_call x1, Pallas kernels, run_experts(): pl.pallas_call(experts_kernel, out_shape=jax.ShapeDtypeStruct(rows.shape,...  3.84 us
  transfers between devices with their start and end apart: 2, of which 2 were waited for; matrix products, arithmetic and copies ran while one was open for 0% of the time, Pallas kernels for 1%

profile of v6, /device:TPU:0, one launch (start us, length us, event | category | flops | bytes accessed | tf_op | source)
XLA Modules:
  0.0 98.0 jit_solution(5564812942767419076)
XLA Ops:
  0.0 0.0 copy-start.5
  0.0 0.0 copy-start.6
  0.0 6.9 %attend.1 = (bf16[16,128,256]{2,1,0:T(8,128)(2,1)}, bf16[128,256]{1,0:T(8,128)(2,1)}) custom-call(s32[1]{0:T(128)} %bitcast.2.head_ref, s32[1]{0:T(128)} %bitcast.3.column_ref, s32[128]{0:T(128)} %lengths_hbm.1, bf16[128,4096]{1,0:T(8,128)(2,1)} %residual_hbm.1, bf16[128,512]{1,0:T(8,128)(2,1)} %query_hbm.1, bf16[128,4,128]{2,1,0:T(4,128)(2,1)} %fresh_key_hbm.1, ...), custom_call_target="tpu_custom_call" | custom-call | tf_op jit(solution)/shard_map/attend/pallas_call | solution.py:138
  6.9 7.1 %all-to-all-start = ((bf16[16,128,256]{2,1,0:T(8,128)(2,1)}), bf16[16,128,256]{2,1,0:T(8,128)(2,1)S(1)}, u32[]{:S(2)}, u32[]{:S(2)}) async-start(bf16[16,128,256]{2,1,0:T(8,128)(2,1)} %get-tuple-element.18), calls=%async_computation | async-start | bytes 2097152 | tf_op jit(solution)/shard_map/all_to_all | solution.py:382
  14.1 0.0 copy-done.5
  14.1 0.0 copy-done.6
  14.1 0.0 copy-start.4
  14.1 0.8 copy-done.4
  14.9 0.2 route.1
  15.1 16.6 %all-to-all-done.pieces_ref = bf16[16,128,256]{2,1,0:T(8,128)(2,1)S(1)} async-done(((bf16[16,128,256]{2,1,0:T(8,128)(2,1)}), bf16[16,128,256]{2,1,0:T(8,128)(2,1)S(1)}, u32[]{:S(2)}, u32[]{:S(2)}) %all-to-all-start) | async-done | bytes 1048608 | tf_op jit(solution)/shard_map/all_to_all | solution.py:382
  31.8 0.0 copy-start
  31.8 0.6 select.5
  32.3 26.1 %all_to_all.20 = bf16[128,16,256]{2,1,0:T(8,128)(2,1)S(1)} all-to-all(bf16[128,16,256]{2,1,0:T(8,128)(2,1)S(1)} %get-tuple-element.20), channel_id=1, replica_groups=mesh['dp'=8,'tensor'=16] {'dp','tensor'}, dimensions={0} | all-to-all | bytes 2097152 | tf_op jit(solution)/shard_map/all_to_all | solution.py:385
  58.5 0.0 copy-done
  58.5 0.0 copy-done.1
  58.5 0.0 copy-done.2
  58.5 0.0 copy-done.3
  58.5 3.8 %experts.1 = bf16[8,16,16,256]{3,2,1,0:T(8,128)(2,1)} custom-call(bf16[8,16,16,256]{3,2,1,0:T(8,128)(2,1)S(1)} %bitcast.18, f32[1,4096]{1,0:T(1,128)S(1)} %bitcast.19, bf16[4096,768]{1,0:T(8,128)(2,1)S(1)} %bitcast.15, bf16[4096,768]{1,0:T(8,128)(2,1)S(1)} %bitcast.16, bf16[768,4096]{1,0:T(8,128)(2,1)S(1)} %bitcast.17), custom_call_target="tpu_custom_call" | custom-call | tf_op jit(solution)/shard_map/experts/pallas_call | solution.py:277
  62.3 4.6 %all-to-all-start.2 = ((bf16[128,16,256]{2,1,0:T(8,128)(2,1)}), bf16[128,16,256]{2,1,0:T(8,128)(2,1)S(1)}, u32[]{:S(2)}, u32[]{:S(2)}) async-start(bf16[128,16,256]{2,1,0:T(8,128)(2,1)} %bitcast.11), calls=%async_computation.2 | async-start | bytes 2097152 | tf_op jit(solution)/shard_map/all_to_all | solution.py:392
  67.0 0.7 spread.1.spread_ref
  67.7 18.4 %all-to-all-done.2.returned_ref = bf16[128,16,256]{2,1,0:T(8,128)(2,1)S(1)} async-done(((bf16[128,16,256]{2,1,0:T(8,128)(2,1)}), bf16[128,16,256]{2,1,0:T(8,128)(2,1)S(1)}, u32[]{:S(2)}, u32[]{:S(2)}) %all-to-all-start.2) | async-done | bytes 1048608 | tf_op jit(solution)/shard_map/all_to_all | solution.py:392
  86.0 0.5 combine.1
  86.5 10.9 %all_to_all.21 = bf16[16,8,256]{2,1,0:T(8,128)(2,1)S(1)} all-to-all(bf16[16,8,256]{2,1,0:T(8,128)(2,1)S(1)} %combine.1), channel_id=1, replica_groups=mesh['dp'=8,'tensor'=16] {'tensor'}, dimensions={0} | all-to-all | bytes 131072 | tf_op jit(solution)/shard_map/all_to_all | solution.py:394
  97.4 0.6 copy.16
  (3 shorter events, 0.0 us)
Async XLA Ops:
  0.0 14.1 %copy-start.5 = (s32[128,8]{0,1:T(8,128)S(1)}, s32[128,8]{0,1:T(8,128)}, u32[]{:S(2)}) copy-start(s32[128,8]{0,1:T(8,128)} %param.23) | copy-start | bytes 12292
  0.0 14.1 %copy-start.6 = (f32[128,8]{0,1:T(8,128)S(1)}, f32[128,8]{0,1:T(8,128)}, u32[]{:S(2)}) copy-start(f32[128,8]{0,1:T(8,128)} %param.24) | copy-start | bytes 12292
  6.9 24.8 %all-to-all-start = ((bf16[16,128,256]{2,1,0:T(8,128)(2,1)}), bf16[16,128,256]{2,1,0:T(8,128)(2,1)S(1)}, u32[]{:S(2)}, u32[]{:S(2)}) async-start(bf16[16,128,256]{2,1,0:T(8,128)(2,1)} %get-tuple-element.18), calls=%async_computation | async-start | bytes 2097152 | tf_op jit(solution)/shard_map/all_to_all | solution.py:382
  14.1 0.8 copy-start.4
  31.8 26.7 %copy-start = (bf16[1,4096,768]{2,1,0:T(8,128)(2,1)S(1)}, bf16[1,4096,768]{2,1,0:T(8,128)(2,1)}, u32[]{:S(2)}) copy-start(bf16[1,4096,768]{2,1,0:T(8,128)(2,1)} %param.25) | copy-start | bytes 18874372
  31.8 26.7 %copy-start.1 = (bf16[1,4096,768]{2,1,0:T(8,128)(2,1)S(1)}, bf16[1,4096,768]{2,1,0:T(8,128)(2,1)}, u32[]{:S(2)}) copy-start(bf16[1,4096,768]{2,1,0:T(8,128)(2,1)} %param.26) | copy-start | bytes 18874372
  31.8 26.7 %copy-start.2 = (bf16[1,768,4096]{2,1,0:T(8,128)(2,1)S(1)}, bf16[1,768,4096]{2,1,0:T(8,128)(2,1)}, u32[]{:S(2)}) copy-start(bf16[1,768,4096]{2,1,0:T(8,128)(2,1)} %param.27) | copy-start | bytes 18874372
  31.8 26.7 %copy-start.3 = (f32[4096]{0:T(1024)S(1)}, f32[4096]{0:T(1024)}, u32[]{:S(2)}) copy-start(f32[4096]{0:T(1024)} %param.22) | copy-start | bytes 49156
  62.3 23.7 %all-to-all-start.2 = ((bf16[128,16,256]{2,1,0:T(8,128)(2,1)}), bf16[128,16,256]{2,1,0:T(8,128)(2,1)S(1)}, u32[]{:S(2)}, u32[]{:S(2)}) async-start(bf16[128,16,256]{2,1,0:T(8,128)(2,1)} %bitcast.11), calls=%async_computation.2 | async-start | bytes 2097152 | tf_op jit(solution)/shard_map/all_to_all | solution.py:392

commit v7 on v6

--- a/solution.py
+++ b/solution.py
@@ -3,7 +3,11 @@
 from jax import lax
 from jax.experimental import pallas as pl
 from jax.experimental.pallas import tpu as pltpu
+from jax.sharding import Mesh
 from jax.sharding import PartitionSpec as P
+
+TENSOR = ("column", "line")
+LINES = 4
 
 
 ROWS_STEP = 32
@@ -244,39 +248,44 @@
     )(pieces, residual, slot)
 
 
-def experts_kernel(rows_ref, gain_ref, gate_ref, up_ref, down_ref, out_ref, normed_ref, act_ref):
+def experts_kernel(rows_ref, gain_ref, gate_ref, up_ref, down_ref, out_ref, gained_ref, act_ref):
     replicas, pieces, slots, chunk = rows_ref.shape
     total = replicas * slots
     width = pieces * chunk
     squares = jnp.zeros((total, chunk), jnp.float32)
     for piece in range(pieces):
         part = rows_ref[:, piece].reshape(total, chunk).astype(jnp.float32)
+        columns = pl.ds(piece * chunk, chunk)
         squares = squares + part * part
+        gained_ref[:, columns] = (part * gain_ref[:, columns]).astype(jnp.bfloat16)
     spread = jnp.sum(squares, axis=-1, keepdims=True) * (1.0 / width)
     scale = lax.rsqrt(spread + 1e-06)
-    for piece in range(pieces):
-        part = rows_ref[:, piece].reshape(total, chunk).astype(jnp.float32)
-        columns = pl.ds(piece * chunk, chunk)
-        normed_ref[:, columns] = (part * scale * gain_ref[:, columns]).astype(jnp.bfloat16)
     for first in range(0, gate_ref.shape[1], chunk):
         units = pl.ds(first, chunk)
-        gate_part = jnp.dot(normed_ref[...], gate_ref[:, units], preferred_element_type=jnp.float32)
-        up_part = jnp.dot(normed_ref[...], up_ref[:, units], preferred_element_type=jnp.float32)
-        act_ref[:, units] = (gate_part / (1.0 + jnp.exp(-gate_part)) * up_part).astype(jnp.bfloat16)
+        gates = scale * jnp.dot(
+            gained_ref[...], gate_ref[:, units], preferred_element_type=jnp.float32
+        )
+        ups = scale * jnp.dot(
+            gained_ref[...], up_ref[:, units], preferred_element_type=jnp.float32
+        )
+        act_ref[:, units] = (gates / (1.0 + jnp.exp(-gates)) * ups).astype(jnp.bfloat16)
     for piece in range(pieces):
         columns = pl.ds(piece * chunk, chunk)
         part = jnp.dot(act_ref[...], down_ref[:, columns], preferred_element_type=jnp.float32)
-        out_ref[:, piece] = part.astype(jnp.bfloat16).reshape(replicas, slots, chunk)
-
-
-def run_experts(rows, norm_gain, weights):
+        block, inner = divmod(piece * chunk, out_ref.shape[3])
+        out_ref[:, block, :, pl.ds(inner, chunk)] = part.astype(jnp.bfloat16).reshape(
+            replicas, slots, chunk
+        )
+
+
+def run_experts(rows, norm_gain, weights, blocks):
     replicas, pieces, slots, chunk = rows.shape
     width, hidden_units = weights[0].shape
     total = replicas * slots
     whole = pl.BlockSpec(memory_space=pltpu.VMEM)
     return pl.pallas_call(
         experts_kernel,
-        out_shape=jax.ShapeDtypeStruct(rows.shape, jnp.bfloat16),
+        out_shape=jax.ShapeDtypeStruct((replicas, blocks, slots, width // blocks), jnp.bfloat16),
         in_specs=[whole] * 5,
         out_specs=whole,
         scratch_shapes=[
@@ -288,23 +297,24 @@
     )(rows, norm_gain.reshape(1, width), *weights)
 
 
-def spread_kernel(slot_ref, weight_ref, spread_ref):
+def spread_kernel(line_ref, slot_ref, weight_ref, spread_ref):
     experts, row_count = slot_ref.shape
     total = spread_ref.shape[2]
-    slots = total // experts
+    slots = total // (experts // LINES)
     step = 256
     slot = slot_ref[...].astype(jnp.float32).T.astype(jnp.bfloat16)
     weight = weight_ref[...].T
     coarse = weight.astype(jnp.bfloat16)
     fine = (weight - coarse.astype(jnp.float32)).astype(jnp.bfloat16)
-    begin = lax.broadcasted_iota(jnp.int32, (experts, step), 0) * slots
-    place = lax.broadcasted_iota(jnp.int32, (experts, step), 1)
-    lane = lax.broadcasted_iota(jnp.int32, (row_count, step), 1)
+    expert = lax.broadcasted_iota(jnp.int32, (experts, step), 0)
+    lane = lax.broadcasted_iota(jnp.int32, (experts, step), 1)
+    row_lane = lax.broadcasted_iota(jnp.int32, (row_count, step), 1)
     for first in range(0, total, step):
-        inside = (place + first >= begin) & (place + first < begin + slots)
-        expand = jnp.where(inside, 1.0, 0.0).astype(jnp.bfloat16)
+        begin = lane + first - lax.rem(lane + first, slots)
+        expand = jnp.where(begin * LINES == (expert - line_ref[0]) * slots, 1.0, 0.0)
+        expand = expand.astype(jnp.bfloat16)
         here = jnp.dot(slot, expand, preferred_element_type=jnp.float32)
-        chosen = here == lax.rem(lane + first, slots).astype(jnp.float32)
+        chosen = here == lax.rem(row_lane + first, slots).astype(jnp.float32)
         for part, values in enumerate((coarse, fine)):
             spread = jnp.dot(values, expand, preferred_element_type=jnp.float32)
             spread_ref[part, :, pl.ds(first, step)] = jnp.where(chosen, spread, 0.0).astype(
@@ -312,40 +322,66 @@
             )
 
 
-def run_spread(slot, row_weight, slots):
+def run_spread(line, slot, row_weight, slots):
     experts, row_count = slot.shape
     whole = pl.BlockSpec(memory_space=pltpu.VMEM)
     return pl.pallas_call(
         spread_kernel,
-        out_shape=jax.ShapeDtypeStruct((2, row_count, experts * slots), jnp.bfloat16),
-        in_specs=[whole] * 2,
+        out_shape=jax.ShapeDtypeStruct((2, row_count, experts // LINES * slots), jnp.bfloat16),
+        in_specs=[pl.BlockSpec(memory_space=pltpu.SMEM), whole, whole],
         out_specs=whole,
         compiler_params=pltpu.CompilerParams(vmem_limit_bytes=4 * 1024 * 1024),
         name="spread",
-    )(slot, row_weight)
-
-
-def combine_kernel(spread_ref, returned_ref, hidden_ref, out_ref):
-    experts, slots, chunk = returned_ref.shape
-    rows = returned_ref[...].reshape(experts * slots, chunk)
-    mixture = jnp.dot(spread_ref[0], rows, preferred_element_type=jnp.float32) + jnp.dot(
+    )(line, slot, row_weight)
+
+
+def combine_kernel(line_ref, spread_ref, returned_ref, hidden_ref, out_ref, sum_ref):
+    experts, slots, width = returned_ref.shape
+    chunk = hidden_ref.shape[1]
+    rows = returned_ref[...].reshape(experts * slots, width)
+    sum_ref[...] = jnp.dot(spread_ref[0], rows, preferred_element_type=jnp.float32) + jnp.dot(
         spread_ref[1], rows, preferred_element_type=jnp.float32
     )
-    layer = hidden_ref[...].astype(jnp.float32) + mixture
-    out_ref[...] = layer.reshape(out_ref.shape).astype(jnp.bfloat16)
-
-
-def run_combine(spread, returned, hidden, parts):
-    row_count, chunk = hidden.shape
+    own = pl.ds(pl.multiple_of(line_ref[0] * chunk, chunk), chunk)
+    sum_ref[:, own] += hidden_ref[...].astype(jnp.float32)
+    out_ref[...] = sum_ref[...].reshape(out_ref.shape).astype(jnp.bfloat16)
+
+
+def run_combine(line, spread, returned, hidden, parts):
+    row_count = hidden.shape[0]
+    width = returned.shape[2]
     whole = pl.BlockSpec(memory_space=pltpu.VMEM)
     return pl.pallas_call(
         combine_kernel,
-        out_shape=jax.ShapeDtypeStruct((parts, row_count // parts, chunk), jnp.bfloat16),
-        in_specs=[whole] * 3,
+        out_shape=jax.ShapeDtypeStruct((parts, row_count // parts, width), jnp.bfloat16),
+        in_specs=[pl.BlockSpec(memory_space=pltpu.SMEM), whole, whole, whole],
+        out_specs=whole,
+        scratch_shapes=[pltpu.VMEM((row_count, width), jnp.float32)],
+        compiler_params=pltpu.CompilerParams(vmem_limit_bytes=8 * 1024 * 1024),
+        name="combine",
+    )(line, spread, returned, hidden)
+
+
+def finish_kernel(parts_ref, out_ref):
+    sources, _, width = parts_ref.shape
+    for block in range(sources // LINES):
+        total = parts_ref[block * LINES].astype(jnp.float32)
+        for line in range(1, LINES):
+            total = total + parts_ref[block * LINES + line].astype(jnp.float32)
+        out_ref[:, pl.ds(block * width, width)] = total.astype(jnp.bfloat16)
+
+
+def run_finish(parts):
+    sources, row_count, width = parts.shape
+    whole = pl.BlockSpec(memory_space=pltpu.VMEM)
+    return pl.pallas_call(
+        finish_kernel,
+        out_shape=jax.ShapeDtypeStruct((row_count, sources // LINES * width), jnp.bfloat16),
+        in_specs=[whole],
         out_specs=whole,
         compiler_params=pltpu.CompilerParams(vmem_limit_bytes=4 * 1024 * 1024),
-        name="combine",
-    )(spread, returned, hidden)
+        name="finish",
+    )(parts)
 
 
 def shards(
@@ -364,12 +400,12 @@
     w_up,
     w_down,
 ):
-    both = ("dp", "tensor")
+    both = ("dp", *TENSOR)
     row_count, width = residual_in.shape
-    tensor_width = lax.axis_size("tensor")
+    tensor_width = lax.axis_size(TENSOR)
     replica_count = lax.axis_size("dp")
     experts_all = replica_count * tensor_width
-    column = lax.axis_index("tensor")
+    column = lax.axis_index(TENSOR)
     chunk = width // tensor_width
     cap_slots = 2 * max(1, row_count * expert_ids.shape[1] // experts_all)
 
@@ -379,45 +415,50 @@
         residual_in, query, fresh_key, fresh_value, key_cache[:, 0], value_cache[:, 0], lengths,
         own_column, kv_head, out_weight, tensor_width,
     )
-    pieces = lax.all_to_all(partial, "tensor", split_axis=0, concat_axis=0, tiled=True)
+    pieces = lax.all_to_all(partial, TENSOR, split_axis=0, concat_axis=0, tiled=True)
     slot, row_weight, residual = run_route(expert_ids, gate_scores, residual, experts_all)
     hidden, outgoing = run_select(pieces, residual, slot, cap_slots)
     received = lax.all_to_all(outgoing, both, split_axis=0, concat_axis=0, tiled=True)
 
     weights = [w_gate[0], w_up[0], w_down[0]]
     rows = received.reshape(replica_count, tensor_width, cap_slots, chunk)
-    answered = run_experts(rows, norm_gain, weights)
-    answered = answered.reshape(experts_all, cap_slots, chunk)
+    answered = run_experts(rows, norm_gain, weights, tensor_width // LINES)
+    answered = answered.reshape(experts_all // LINES, cap_slots, width // (tensor_width // LINES))
     slot, row_weight, answered = lax.optimization_barrier((slot, row_weight, answered))
-    returned = lax.all_to_all(answered, both, split_axis=0, concat_axis=0, tiled=True)
-    spread = run_spread(slot, row_weight, cap_slots)
+    returned = lax.all_to_all(
+        answered, ("dp", "column"), split_axis=0, concat_axis=0, tiled=True
+    )
+    line = lax.axis_index("line").astype(jnp.int32).reshape(1)
+    spread = run_spread(line, slot, row_weight, cap_slots)
     own = lax.all_to_all(
-        run_combine(spread, returned, hidden, tensor_width),
-        "tensor",
+        run_combine(line, spread, returned, hidden, tensor_width),
+        TENSOR,
         split_axis=0,
         concat_axis=0,
         tiled=True,
     )
-    return own.transpose(1, 0, 2).reshape(row_count // tensor_width, width)
+    return run_finish(own)
 
 
 def solution(mesh):
+    shape = (mesh.shape["dp"], mesh.shape["tensor"] // LINES, LINES)
+    mesh = Mesh(mesh.devices.reshape(shape), ("dp", *TENSOR))
     placed = (
         P("dp", None),
-        P("dp", "tensor"),
+        P("dp", TENSOR),
         P("dp", None, None),
         P("dp", None, None),
-        P("dp", "tensor", None, None),
-        P("dp", "tensor", None, None),
+        P("dp", TENSOR, None, None),
+        P("dp", TENSOR, None, None),
         P("dp"),
-        P("tensor", None),
+        P(TENSOR, None),
         P(),
         P("dp", None),
         P("dp", None),
-        P(("dp", "tensor"), None, None),
-        P(("dp", "tensor"), None, None),
-        P(("dp", "tensor"), None, None),
+        P(("dp", *TENSOR), None, None),
+        P(("dp", *TENSOR), None, None),
+        P(("dp", *TENSOR), None, None),
     )
     return jax.shard_map(
-        shards, mesh=mesh, in_specs=placed, out_specs=P(("dp", "tensor"), None), check_vma=False
-    )
+        shards, mesh=mesh, in_specs=placed, out_specs=P(("dp", *TENSOR), None), check_vma=False
+    )

time: 98.3 us -> 96.3 us (0.980)
  waiting for transfers between devices: 35 us -> 33.4 us
    all_to_all x2, waiting for transfers between devices: 35 us -> 33.4 us  [the longest x1 16.7 us: shards(): lax.all_to_all(answered, ('dp', 'column'), split_axis=0, concat_axis=0, t...]
    pallas_call x1 -> x2, Pallas kernels: 3.84 us -> 4.36 us  [the longest x1 3.7 us: run_experts(): pl.pallas_call(experts_kernel, out_shape=jax.ShapeDtypeStruct((replicas,...]
where the time goes in v7:
time: 96.3 us; the launch traced here: 96 us
  blocking collectives  37.8 us (39%)
  waiting for transfers between devices  33.4 us (35%)
  Pallas kernels  12.8 us (13%)
  starting transfers between devices  11.1 us (12%)
    all_to_all x1, blocking collectives, shards(): lax.all_to_all(outgoing, both, split_axis=0, concat_axis=0, tiled=True)  26.1 us
    all_to_all x1, waiting for transfers between devices, shards(): lax.all_to_all(answered, ('dp', 'column'), split_axis=0, concat_axis=0, t...  16.7 us
    all_to_all x1, waiting for transfers between devices, shards(): lax.all_to_all(partial, TENSOR, split_axis=0, concat_axis=0, tiled=True)  16.6 us
    all_to_all x1, blocking collectives, shards(): lax.all_to_all(run_combine(line, spread, returned, hidden, tensor_width),...  11.6 us
    all_to_all x1, starting transfers between devices, shards(): lax.all_to_all(partial, TENSOR, split_axis=0, concat_axis=0, tiled=True)  7.13 us
    pallas_call x1, Pallas kernels, run_attend(): pl.pallas_call(attend_kernel, out_shape=(jax.ShapeDtypeStruct((pieces, ro...  6.9 us
    all_to_all x1, starting transfers between devices, shards(): lax.all_to_all(answered, ('dp', 'column'), split_axis=0, concat_axis=0, t...  3.93 us
    pallas_call x1, Pallas kernels, run_experts(): pl.pallas_call(experts_kernel, out_shape=jax.ShapeDtypeStruct((replicas,...  3.7 us
  transfers between devices with their start and end apart: 2, of which 2 were waited for; matrix products, arithmetic and copies ran while one was open for 0% of the time, Pallas kernels for 1%

profile of v7, /device:TPU:0, one launch (start us, length us, event | category | flops | bytes accessed | tf_op | source)
XLA Modules:
  0.0 96.0 jit_solution(10538356028223097744)
XLA Ops:
  0.0 0.0 copy-start.5
  0.0 0.0 copy-start.6
  0.0 6.9 %attend.1 = (bf16[16,128,256]{2,1,0:T(8,128)(2,1)}, bf16[128,256]{1,0:T(8,128)(2,1)}) custom-call(s32[1]{0:T(128)} %bitcast.3.head_ref, s32[1]{0:T(128)} %bitcast.4.column_ref, s32[128]{0:T(128)} %lengths_hbm.1, bf16[128,4096]{1,0:T(8,128)(2,1)} %residual_hbm.1, bf16[128,512]{1,0:T(8,128)(2,1)} %query_hbm.1, bf16[128,4,128]{2,1,0:T(4,128)(2,1)} %fresh_key_hbm.1, ...), custom_call_target="tpu_custom_call" | custom-call | tf_op jit(solution)/shard_map/attend/pallas_call | solution.py:142
  6.9 7.1 %all-to-all-start = ((bf16[16,128,256]{2,1,0:T(8,128)(2,1)}), bf16[16,128,256]{2,1,0:T(8,128)(2,1)S(1)}, u32[]{:S(2)}, u32[]{:S(2)}) async-start(bf16[16,128,256]{2,1,0:T(8,128)(2,1)} %get-tuple-element.18), calls=%async_computation | async-start | bytes 2097152 | tf_op jit(solution)/shard_map/all_to_all | solution.py:418
  14.1 0.0 copy-done.5
  14.1 0.0 copy-done.6
  14.1 0.0 copy-start.4
  14.1 0.8 copy-done.4
  14.9 0.2 route.1
  15.1 16.6 %all-to-all-done.pieces_ref = bf16[16,128,256]{2,1,0:T(8,128)(2,1)S(1)} async-done(((bf16[16,128,256]{2,1,0:T(8,128)(2,1)}), bf16[16,128,256]{2,1,0:T(8,128)(2,1)S(1)}, u32[]{:S(2)}, u32[]{:S(2)}) %all-to-all-start) | async-done | bytes 1048608 | tf_op jit(solution)/shard_map/all_to_all | solution.py:418
  31.8 0.0 copy-start
  31.8 0.6 select.5
  32.3 26.1 %all_to_all.20 = bf16[128,16,256]{2,1,0:T(8,128)(2,1)S(1)} all-to-all(bf16[128,16,256]{2,1,0:T(8,128)(2,1)S(1)} %get-tuple-element.20), channel_id=1, replica_groups=mesh['dp'=8,'column'=4,'line'=4] {'dp','column','line'}, dimensions={0} | all-to-all | bytes 2097152 | tf_op jit(solution)/shard_map/all_to_all | solution.py:421
  58.5 0.0 copy-done
  58.5 0.0 copy-done.1
  58.5 0.0 copy-done.2
  58.5 0.0 copy-done.3
  58.5 3.7 %experts.1 = bf16[8,4,16,1024]{3,2,1,0:T(8,128)(2,1)} custom-call(bf16[8,16,16,256]{3,2,1,0:T(8,128)(2,1)S(1)} %bitcast.16, f32[1,4096]{1,0:T(1,128)S(1)} %bitcast.17, bf16[4096,768]{1,0:T(8,128)(2,1)S(1)} %bitcast.13, bf16[4096,768]{1,0:T(8,128)(2,1)S(1)} %bitcast.14, bf16[768,4096]{1,0:T(8,128)(2,1)S(1)} %bitcast.15), custom_call_target="tpu_custom_call" | custom-call | tf_op jit(solution)/shard_map/experts/pallas_call | solution.py:286
  62.2 3.9 %all-to-all-start.2 = ((bf16[32,16,1024]{2,1,0:T(8,128)(2,1)}), bf16[32,16,1024]{2,1,0:T(8,128)(2,1)S(1)}, u32[]{:S(2)}, u32[]{:S(2)}) async-start(bf16[32,16,1024]{2,1,0:T(8,128)(2,1)} %bitcast.12), calls=%async_computation.2 | async-start | bytes 2097152 | tf_op jit(solution)/shard_map/all_to_all | solution.py:428
  66.1 0.3 spread.1.spread_ref
  66.4 16.7 %all-to-all-done.2.returned_ref = bf16[32,16,1024]{2,1,0:T(8,128)(2,1)S(1)} async-done(((bf16[32,16,1024]{2,1,0:T(8,128)(2,1)}), bf16[32,16,1024]{2,1,0:T(8,128)(2,1)S(1)}, u32[]{:S(2)}, u32[]{:S(2)}) %all-to-all-start.2) | async-done | bytes 1048608 | tf_op jit(solution)/shard_map/all_to_all | solution.py:428
  83.2 0.5 combine.1
  83.7 11.6 %all_to_all.21.parts_ref = bf16[16,8,1024]{2,1,0:T(8,128)(2,1)S(1)} all-to-all(bf16[16,8,1024]{2,1,0:T(8,128)(2,1)S(1)} %combine.1), channel_id=1, replica_groups=mesh['dp'=8,'column'=4,'line'=4] {'column','line'}, dimensions={0} | all-to-all | bytes 524288 | tf_op jit(solution)/shard_map/all_to_all | solution.py:433
  95.3 0.7 finish.1
  (3 shorter events, 0.0 us)
Async XLA Ops:
  0.0 14.1 %copy-start.5 = (s32[128,8]{0,1:T(8,128)S(1)}, s32[128,8]{0,1:T(8,128)}, u32[]{:S(2)}) copy-start(s32[128,8]{0,1:T(8,128)} %param.23) | copy-start | bytes 12292
  0.0 14.1 %copy-start.6 = (f32[128,8]{0,1:T(8,128)S(1)}, f32[128,8]{0,1:T(8,128)}, u32[]{:S(2)}) copy-start(f32[128,8]{0,1:T(8,128)} %param.24) | copy-start | bytes 12292
  6.9 24.8 %all-to-all-start = ((bf16[16,128,256]{2,1,0:T(8,128)(2,1)}), bf16[16,128,256]{2,1,0:T(8,128)(2,1)S(1)}, u32[]{:S(2)}, u32[]{:S(2)}) async-start(bf16[16,128,256]{2,1,0:T(8,128)(2,1)} %get-tuple-element.18), calls=%async_computation | async-start | bytes 2097152 | tf_op jit(solution)/shard_map/all_to_all | solution.py:418
  14.1 0.8 copy-start.4
  31.8 26.7 %copy-start = (bf16[1,4096,768]{2,1,0:T(8,128)(2,1)S(1)}, bf16[1,4096,768]{2,1,0:T(8,128)(2,1)}, u32[]{:S(2)}) copy-start(bf16[1,4096,768]{2,1,0:T(8,128)(2,1)} %param.25) | copy-start | bytes 18874372
  31.8 26.7 %copy-start.1 = (bf16[1,4096,768]{2,1,0:T(8,128)(2,1)S(1)}, bf16[1,4096,768]{2,1,0:T(8,128)(2,1)}, u32[]{:S(2)}) copy-start(bf16[1,4096,768]{2,1,0:T(8,128)(2,1)} %param.26) | copy-start | bytes 18874372
  31.8 26.7 %copy-start.2 = (bf16[1,768,4096]{2,1,0:T(8,128)(2,1)S(1)}, bf16[1,768,4096]{2,1,0:T(8,128)(2,1)}, u32[]{:S(2)}) copy-start(bf16[1,768,4096]{2,1,0:T(8,128)(2,1)} %param.27) | copy-start | bytes 18874372
  31.8 26.7 %copy-start.3 = (f32[4096]{0:T(1024)S(1)}, f32[4096]{0:T(1024)}, u32[]{:S(2)}) copy-start(f32[4096]{0:T(1024)} %param.22) | copy-start | bytes 49156
  62.2 21.0 %all-to-all-start.2 = ((bf16[32,16,1024]{2,1,0:T(8,128)(2,1)}), bf16[32,16,1024]{2,1,0:T(8,128)(2,1)S(1)}, u32[]{:S(2)}, u32[]{:S(2)}) async-start(bf16[32,16,1024]{2,1,0:T(8,128)(2,1)} %bitcast.12), calls=%async_computation.2 | async-start | bytes 2097152 | tf_op jit(solution)/shard_map/all_to_all | solution.py:428

commit v8 on v7

--- a/solution.py
+++ b/solution.py
@@ -248,10 +248,16 @@
     )(pieces, residual, slot)
 
 
-def experts_kernel(rows_ref, gain_ref, gate_ref, up_ref, down_ref, out_ref, gained_ref, act_ref):
+def experts_kernel(
+    rows_ref, gain_ref, gate_ref, up_ref, down_ref, out_hbm, gained_ref, act_ref, out_ref, out_sem
+):
     replicas, pieces, slots, chunk = rows_ref.shape
     total = replicas * slots
     width = pieces * chunk
+
+    def out_copy(block):
+        return pltpu.make_async_copy(out_ref.at[:, block], out_hbm.at[:, block], out_sem.at[block])
+
     squares = jnp.zeros((total, chunk), jnp.float32)
     for piece in range(pieces):
         part = rows_ref[:, piece].reshape(total, chunk).astype(jnp.float32)
@@ -276,6 +282,10 @@
         out_ref[:, block, :, pl.ds(inner, chunk)] = part.astype(jnp.bfloat16).reshape(
             replicas, slots, chunk
         )
+        if inner + chunk == out_ref.shape[3]:
+            out_copy(block).start()
+    for block in range(out_ref.shape[1]):
+        out_copy(block).wait()
 
 
 def run_experts(rows, norm_gain, weights, blocks):
@@ -287,10 +297,12 @@
         experts_kernel,
         out_shape=jax.ShapeDtypeStruct((replicas, blocks, slots, width // blocks), jnp.bfloat16),
         in_specs=[whole] * 5,
-        out_specs=whole,
+        out_specs=pl.BlockSpec(memory_space=pltpu.HBM),
         scratch_shapes=[
             pltpu.VMEM((total, width), jnp.bfloat16),
             pltpu.VMEM((total, hidden_units), jnp.bfloat16),
+            pltpu.VMEM((replicas, blocks, slots, width // blocks), jnp.bfloat16),
+            pltpu.SemaphoreType.DMA((blocks,)),
         ],
         compiler_params=pltpu.CompilerParams(vmem_limit_bytes=16 * 1024 * 1024),
         name="experts",

time: 96.3 us -> 96.1 us (level)
  no operation moved by 1% of the time
where the time goes in v8:
time: 96.1 us; the launch traced here: 95.8 us
  blocking collectives  37.8 us (39%)
  waiting for transfers between devices  33.4 us (35%)
  Pallas kernels  12.6 us (13%)
  starting transfers between devices  11.1 us (12%)
    all_to_all x1, blocking collectives, shards(): lax.all_to_all(outgoing, both, split_axis=0, concat_axis=0, tiled=True)  26.1 us
    all_to_all x1, waiting for transfers between devices, shards(): lax.all_to_all(answered, ('dp', 'column'), split_axis=0, concat_axis=0, t...  16.7 us
    all_to_all x1, waiting for transfers between devices, shards(): lax.all_to_all(partial, TENSOR, split_axis=0, concat_axis=0, tiled=True)  16.6 us
    all_to_all x1, blocking collectives, shards(): lax.all_to_all(run_combine(line, spread, returned, hidden, tensor_width),...  11.6 us
    all_to_all x1, starting transfers between devices, shards(): lax.all_to_all(partial, TENSOR, split_axis=0, concat_axis=0, tiled=True)  7.13 us
    pallas_call x1, Pallas kernels, run_attend(): pl.pallas_call(attend_kernel, out_shape=(jax.ShapeDtypeStruct((pieces, ro...  6.9 us
    all_to_all x1, starting transfers between devices, shards(): lax.all_to_all(answered, ('dp', 'column'), split_axis=0, concat_axis=0, t...  3.94 us
    pallas_call x1, Pallas kernels, run_experts(): pl.pallas_call(experts_kernel, out_shape=jax.ShapeDtypeStruct((replicas,...  3.47 us
  transfers between devices with their start and end apart: 2, of which 2 were waited for; matrix products, arithmetic and copies ran while one was open for 0% of the time, Pallas kernels for 1%

profile of v8, /device:TPU:0, one launch (start us, length us, event | category | flops | bytes accessed | tf_op | source)
XLA Modules:
  0.0 95.8 jit_solution(10206814696251784803)
XLA Ops:
  0.0 0.0 copy-start.5
  0.0 0.0 copy-start.6
  0.0 6.9 %attend.1 = (bf16[16,128,256]{2,1,0:T(8,128)(2,1)}, bf16[128,256]{1,0:T(8,128)(2,1)}) custom-call(s32[1]{0:T(128)} %bitcast.3.head_ref, s32[1]{0:T(128)} %bitcast.4.column_ref, s32[128]{0:T(128)} %lengths_hbm.1, bf16[128,4096]{1,0:T(8,128)(2,1)} %residual_hbm.1, bf16[128,512]{1,0:T(8,128)(2,1)} %query_hbm.1, bf16[128,4,128]{2,1,0:T(4,128)(2,1)} %fresh_key_hbm.1, ...), custom_call_target="tpu_custom_call" | custom-call | tf_op jit(solution)/shard_map/attend/pallas_call | solution.py:142
  6.9 7.1 %all-to-all-start = ((bf16[16,128,256]{2,1,0:T(8,128)(2,1)}), bf16[16,128,256]{2,1,0:T(8,128)(2,1)S(1)}, u32[]{:S(2)}, u32[]{:S(2)}) async-start(bf16[16,128,256]{2,1,0:T(8,128)(2,1)} %get-tuple-element.18), calls=%async_computation | async-start | bytes 2097152 | tf_op jit(solution)/shard_map/all_to_all | solution.py:430
  14.1 0.0 copy-done.5
  14.1 0.0 copy-done.6
  14.1 0.0 copy-start.4
  14.1 0.8 copy-done.4
  14.9 0.2 route.1
  15.1 16.6 %all-to-all-done.pieces_ref = bf16[16,128,256]{2,1,0:T(8,128)(2,1)S(1)} async-done(((bf16[16,128,256]{2,1,0:T(8,128)(2,1)}), bf16[16,128,256]{2,1,0:T(8,128)(2,1)S(1)}, u32[]{:S(2)}, u32[]{:S(2)}) %all-to-all-start) | async-done | bytes 1048608 | tf_op jit(solution)/shard_map/all_to_all | solution.py:430
  31.8 0.0 copy-start
  31.8 0.6 select.5
  32.3 26.1 %all_to_all.20 = bf16[128,16,256]{2,1,0:T(8,128)(2,1)S(1)} all-to-all(bf16[128,16,256]{2,1,0:T(8,128)(2,1)S(1)} %get-tuple-element.20), channel_id=1, replica_groups=mesh['dp'=8,'column'=4,'line'=4] {'dp','column','line'}, dimensions={0} | all-to-all | bytes 2097152 | tf_op jit(solution)/shard_map/all_to_all | solution.py:433
  58.5 0.0 copy-done
  58.5 0.0 copy-done.1
  58.5 0.0 copy-done.2
  58.5 0.0 copy-done.3
  58.5 3.5 %experts.1 = bf16[8,4,16,1024]{3,2,1,0:T(8,128)(2,1)} custom-call(bf16[8,16,16,256]{3,2,1,0:T(8,128)(2,1)S(1)} %bitcast.16, f32[1,4096]{1,0:T(1,128)S(1)} %bitcast.17, bf16[4096,768]{1,0:T(8,128)(2,1)S(1)} %bitcast.13, bf16[4096,768]{1,0:T(8,128)(2,1)S(1)} %bitcast.14, bf16[768,4096]{1,0:T(8,128)(2,1)S(1)} %bitcast.15), custom_call_target="tpu_custom_call" | custom-call | tf_op jit(solution)/shard_map/experts/pallas_call | solution.py:296
  62.0 3.9 %all-to-all-start.2 = ((bf16[32,16,1024]{2,1,0:T(8,128)(2,1)}), bf16[32,16,1024]{2,1,0:T(8,128)(2,1)S(1)}, u32[]{:S(2)}, u32[]{:S(2)}) async-start(bf16[32,16,1024]{2,1,0:T(8,128)(2,1)} %bitcast.12), calls=%async_computation.2 | async-start | bytes 2097152 | tf_op jit(solution)/shard_map/all_to_all | solution.py:440
  65.9 0.3 spread.1.spread_ref
  66.2 16.7 %all-to-all-done.2.returned_ref = bf16[32,16,1024]{2,1,0:T(8,128)(2,1)S(1)} async-done(((bf16[32,16,1024]{2,1,0:T(8,128)(2,1)}), bf16[32,16,1024]{2,1,0:T(8,128)(2,1)S(1)}, u32[]{:S(2)}, u32[]{:S(2)}) %all-to-all-start.2) | async-done | bytes 1048608 | tf_op jit(solution)/shard_map/all_to_all | solution.py:440
  83.0 0.5 combine.1
  83.5 11.6 %all_to_all.21.parts_ref = bf16[16,8,1024]{2,1,0:T(8,128)(2,1)S(1)} all-to-all(bf16[16,8,1024]{2,1,0:T(8,128)(2,1)S(1)} %combine.1), channel_id=1, replica_groups=mesh['dp'=8,'column'=4,'line'=4] {'column','line'}, dimensions={0} | all-to-all | bytes 524288 | tf_op jit(solution)/shard_map/all_to_all | solution.py:445
  95.1 0.7 finish.1
  (3 shorter events, 0.0 us)
Async XLA Ops:
  0.0 14.1 %copy-start.5 = (s32[128,8]{0,1:T(8,128)S(1)}, s32[128,8]{0,1:T(8,128)}, u32[]{:S(2)}) copy-start(s32[128,8]{0,1:T(8,128)} %param.23) | copy-start | bytes 12292
  0.0 14.1 %copy-start.6 = (f32[128,8]{0,1:T(8,128)S(1)}, f32[128,8]{0,1:T(8,128)}, u32[]{:S(2)}) copy-start(f32[128,8]{0,1:T(8,128)} %param.24) | copy-start | bytes 12292
  6.9 24.8 %all-to-all-start = ((bf16[16,128,256]{2,1,0:T(8,128)(2,1)}), bf16[16,128,256]{2,1,0:T(8,128)(2,1)S(1)}, u32[]{:S(2)}, u32[]{:S(2)}) async-start(bf16[16,128,256]{2,1,0:T(8,128)(2,1)} %get-tuple-element.18), calls=%async_computation | async-start | bytes 2097152 | tf_op jit(solution)/shard_map/all_to_all | solution.py:430
  14.1 0.8 copy-start.4
  31.8 26.7 %copy-start = (bf16[1,4096,768]{2,1,0:T(8,128)(2,1)S(1)}, bf16[1,4096,768]{2,1,0:T(8,128)(2,1)}, u32[]{:S(2)}) copy-start(bf16[1,4096,768]{2,1,0:T(8,128)(2,1)} %param.25) | copy-start | bytes 18874372
  31.8 26.7 %copy-start.1 = (bf16[1,4096,768]{2,1,0:T(8,128)(2,1)S(1)}, bf16[1,4096,768]{2,1,0:T(8,128)(2,1)}, u32[]{:S(2)}) copy-start(bf16[1,4096,768]{2,1,0:T(8,128)(2,1)} %param.26) | copy-start | bytes 18874372
  31.8 26.7 %copy-start.2 = (bf16[1,768,4096]{2,1,0:T(8,128)(2,1)S(1)}, bf16[1,768,4096]{2,1,0:T(8,128)(2,1)}, u32[]{:S(2)}) copy-start(bf16[1,768,4096]{2,1,0:T(8,128)(2,1)} %param.27) | copy-start | bytes 18874372
  31.8 26.7 %copy-start.3 = (f32[4096]{0:T(1024)S(1)}, f32[4096]{0:T(1024)}, u32[]{:S(2)}) copy-start(f32[4096]{0:T(1024)} %param.22) | copy-start | bytes 49156
  62.0 21.0 %all-to-all-start.2 = ((bf16[32,16,1024]{2,1,0:T(8,128)(2,1)}), bf16[32,16,1024]{2,1,0:T(8,128)(2,1)S(1)}, u32[]{:S(2)}, u32[]{:S(2)}) async-start(bf16[32,16,1024]{2,1,0:T(8,128)(2,1)} %bitcast.12), calls=%async_computation.2 | async-start | bytes 2097152 | tf_op jit(solution)/shard_map/all_to_all | solution.py:440
